TPU v7x, 256 devices: a whole 4x4x8 slice. The times are simulated.
256 devices in a mesh: dp: 32 (over y, x, z_hi), tensor: 8 (over z_lo, core).
Axes of the slice: x: 4, y: 4, z: 8 (z_hi: 2, z_lo: 4; z = z_hi * 4 + z_lo), core: 2. Of those that a mesh axis runs over, the one named last changes fastest.
Arguments:
- leaf_tokens: bfloat16 [512, 8, 2048], P(('dp', 'tensor')), may hold values from -40 to 40
- attn_gain: float32 [2048], replicated, may hold values from 0.25 to 2.5
- w_query: bfloat16 [2048, 2048], P(None, 'tensor'), may hold values from -0.125 to 0.125
- w_key: bfloat16 [2048, 2048], P(None, 'tensor'), may hold values from -0.125 to 0.125
- w_value: bfloat16 [2048, 2048], P(None, 'tensor'), may hold values from -0.125 to 0.125
- w_out: bfloat16 [2048, 2048], P('tensor'), may hold values from -0.125 to 0.125
- prefix_kv: bfloat16 [2, 28672, 2048], P(None, 'dp', 'tensor'), may hold values from -104 to 104
- prefix_owner: int32 [512, 3], P('dp'), may hold values from 0 to 31, as said below
- prefix_start: int32 [512, 3], P('dp'), may hold values from 0 to 864, as said below
- prefix_len: int32 [512, 3], P('dp'), may hold values from 1 to 512, as said below
- mlp_gain: float32 [2048], replicated, may hold values from 0.25 to 2.5
- shared_in: bfloat16 [2048, 2, 1408], P(None, None, 'tensor'), may hold values from -0.125 to 0.125
- shared_out: bfloat16 [1408, 2048], P('tensor'), may hold values from -0.15625 to 0.15625
- expert_in: bfloat16 [64, 2048, 2, 1408], P('dp', None, None, 'tensor'), may hold values from -0.125 to 0.125
- expert_out: bfloat16 [64, 1408, 2048], P('dp', 'tensor'), may hold values from -0.15625 to 0.15625
- expert_ids: int32 [512, 8, 6], P('dp'), may hold values from 0 to 63, all different within a row; in each aligned block of 128 rows (0 to 127, 128 to 255, ..., all dimensions but the last counted through in order) at most 16 rows name the same one
- gate_weights: float32 [512, 8, 6], P('dp'), may hold values from 0.05 to 0.4
- request_of: int32 [512], P('dp'), may hold values from 0 to 511, as said below
Outputs:
- layer_out: bfloat16 [512, 8, 2048], P('dp', 'tensor')
Inputs may be any that keep to these rules, and one draw needn't show every extreme that they name: `prefix_owner`: each data group owns exactly one first-level node, two second-level nodes and four third-level nodes; a first-level node serves 16 requests, a second-level node half as many, a third-level node a quarter. The 16 requests of one data group name 16 different owners at each level, and together over the three levels they name no owner more than twice. `prefix_start`: the first level starts at 0; the second at 512 or 640; the third at 768 + q * 32 with q from 0 to 3. `prefix_len`: A node has 1 to 512, 128 or 32 keys at the first, second or third level, each of these maxima reached. Requests naming the same owner and start at a level share that node and its length; each node lies under one node of the level above. `expert_ids`: each row names 6 different experts; in the rows of one data group (aligned blocks of 128 rows) no expert is named more than 16 times. `request_of`: A permutation; the 16 dealt requests of one data group go to 16 different data groups.
All inputs are finite; a program needn't handle non-finite values.
Results may differ from a plain program's by a relative error of at most 0.025.
Values may be sent and summed in bfloat16 or wider, within the bound.
A program may use at most 128 MiB of HBM per device.

v0:
```python
import jax
import jax.numpy as jnp
from jax import lax
from jax.sharding import PartitionSpec as P

HEAD_DIM = 128


EPS = 1e-06
ROPE_BASE = 10000.0


def rms_scaled(values, gain_vector):
    mean_square = jnp.mean(values * values, axis=-1, keepdims=True)
    return values * lax.rsqrt(mean_square + EPS) * gain_vector


def rotate_heads(values, positions):
    head_dim = values.shape[-1]
    half_dim = head_dim // 2
    frequency = ROPE_BASE ** (-2.0 * jnp.arange(half_dim, dtype=jnp.float32) / head_dim)
    angles = positions[..., None, None] * frequency
    cosine = jnp.cos(angles)
    sine_part = jnp.sin(angles)
    first_half = values[..., :half_dim]
    second_half = values[..., half_dim:]
    return jnp.concatenate(
        [
            first_half * cosine - second_half * sine_part,
            second_half * cosine + first_half * sine_part,
        ],
        axis=-1,
    )


def softmax_parts(scores, visible):
    scores = jnp.where(visible, scores, -jnp.inf)
    highest = jnp.max(scores, axis=-1, keepdims=True)
    anchor = jnp.where(jnp.isfinite(highest), highest, 0.0)
    weights = jnp.exp(scores - anchor)
    totals = jnp.sum(weights, axis=-1, keepdims=True)
    return (weights, anchor, totals)


def merge_parts(outputs, log_totals):
    stacked = jnp.stack(log_totals, axis=0)
    highest = jnp.max(stacked, axis=0)
    scales = jnp.exp(stacked - highest)
    weighted = scales[0][..., None] * outputs[0]
    for part_index in range(1, len(outputs)):
        weighted = weighted + scales[part_index][..., None] * outputs[part_index]
    return weighted / jnp.sum(scales, axis=0)[..., None]


def owner_parts(shipped, shipped_meta, pool_keys, pool_values, score_scale):
    source_count, item_count, leaf_len, local_width = shipped.shape
    local_heads = pool_keys.shape[1]
    head_dim = pool_keys.shape[2]
    query_rows = shipped.reshape(source_count * item_count * leaf_len, local_heads, head_dim)
    scores = (
        jnp.einsum("qhd,khd->qhk", query_rows, pool_keys, preferred_element_type=jnp.float32)
        * score_scale
    )
    first_key = jnp.repeat(shipped_meta[..., 0].reshape(-1), leaf_len)
    key_count = jnp.repeat(shipped_meta[..., 1].reshape(-1), leaf_len)
    key_place = jnp.arange(pool_keys.shape[0])
    visible = (key_place[None, :] >= first_key[:, None]) & (
        key_place[None, :] < (first_key + key_count)[:, None]
    )
    weights, anchor, totals = softmax_parts(scores, visible[:, None, :])
    guarded = jnp.maximum(totals, 1.0)
    mixed_part = (
        jnp.einsum(
            "qhk,khd->qhd",
            weights.astype(jnp.bfloat16),
            pool_values,
            preferred_element_type=jnp.float32,
        )
        / guarded
    )
    log_part = (anchor + jnp.log(guarded))[..., 0]
    return (
        mixed_part.reshape(source_count, item_count, leaf_len, local_width),
        log_part.reshape(source_count, item_count, leaf_len, local_heads),
    )


def expert_partial(arrived, weight_in, weight_back, groups):
    local_experts = weight_in.shape[0]
    slot_count = arrived.shape[1]
    model_width = arrived.shape[2]
    grouped = arrived.reshape(groups, local_experts, slot_count, model_width)
    gate_up = jnp.einsum("sekd,edf->sekf", grouped, weight_in, preferred_element_type=jnp.float32)
    half_width = gate_up.shape[-1] // 2
    acted = (jax.nn.silu(gate_up[..., :half_width]) * gate_up[..., half_width:]).astype(
        jnp.bfloat16
    )
    partial_value = jnp.einsum(
        "sekf,efd->sekd", acted, weight_back, preferred_element_type=jnp.float32
    )
    return partial_value.astype(jnp.bfloat16).reshape(
        groups * local_experts, slot_count, model_width
    )


def on_device(
    leaf_tokens,
    attn_gain,
    w_query,
    w_key,
    w_value,
    w_out,
    prefix_kv,
    prefix_owner,
    prefix_start,
    prefix_len,
    mlp_gain,
    shared_in,
    shared_out,
    expert_in,
    expert_out,
    expert_ids,
    gate_weights,
    request_of,
):
    groups = lax.axis_size("dp")
    tensors = lax.axis_size("tensor")
    shard_requests, leaf_len, model_width = leaf_tokens.shape
    group_requests = prefix_owner.shape[0]
    local_width = w_query.shape[1]
    head_dim = HEAD_DIM
    local_heads = local_width // head_dim
    score_scale = head_dim ** (-0.5)
    owner_ids = jnp.arange(groups)
    residual = leaf_tokens.astype(jnp.float32)
    normed_attn = rms_scaled(residual, attn_gain).astype(jnp.bfloat16)
    offsets = jnp.sum(prefix_len, axis=1).astype(jnp.float32)
    shard_rows = lax.all_gather(normed_attn, "tensor", axis=0, tiled=True)
    row_count = shard_rows.shape[0]
    positions = offsets[:, None] + jnp.arange(leaf_len, dtype=jnp.float32)[None, :]
    columns = []
    for weight in (w_query, w_key):
        product = jnp.einsum("ald,dk->alk", shard_rows, weight, preferred_element_type=jnp.float32)
        product = rotate_heads(
            product.reshape(row_count, leaf_len, local_heads, head_dim), positions
        )
        columns.append(product.reshape(row_count, leaf_len, local_width))
    columns.append(
        jnp.einsum("ald,dk->alk", shard_rows, w_value, preferred_element_type=jnp.float32)
    )
    projected = jnp.concatenate(columns, axis=-1).astype(jnp.bfloat16)
    query_flat = projected[..., :local_width]
    queries = query_flat.reshape(group_requests, leaf_len, local_heads, head_dim)
    key_rows = projected[..., local_width : 2 * local_width].reshape(
        group_requests, leaf_len, local_heads, head_dim
    )
    leaf_values = projected[..., 2 * local_width :].reshape(
        group_requests, leaf_len, local_heads, head_dim
    )
    scores = (
        jnp.einsum("rihd,rjhd->rhij", queries, key_rows, preferred_element_type=jnp.float32)
        * score_scale
    )
    causal = jnp.arange(leaf_len)[:, None] >= jnp.arange(leaf_len)[None, :]
    weights, anchor, totals = softmax_parts(scores, causal[None, None])
    mixed_leaf = jnp.einsum(
        "rhij,rjhd->rihd",
        weights.astype(jnp.bfloat16),
        leaf_values,
        preferred_element_type=jnp.float32,
    )
    outputs = [mixed_leaf / jnp.transpose(totals, (0, 2, 1, 3))]
    log_totals = [jnp.transpose(anchor + jnp.log(totals), (0, 2, 1, 3))[..., 0]]
    pool_keys = prefix_kv[0].reshape(-1, local_heads, head_dim)
    pool_values = prefix_kv[1].reshape(-1, local_heads, head_dim)
    node_meta = jnp.stack([prefix_start, prefix_len], axis=-1)
    for tree_level in range(3):
        targets = prefix_owner[:, tree_level]
        placing = targets[:, None] == owner_ids[None, :]
        shipped = jnp.einsum(
            "ag,ald->gld",
            placing.astype(jnp.bfloat16),
            query_flat,
            preferred_element_type=jnp.float32,
        ).astype(jnp.bfloat16)
        shipped_meta = jnp.sum(
            placing.astype(jnp.int32)[:, :, None] * node_meta[:, tree_level, None, :], axis=0
        )
        mixed_part, log_part = owner_parts(
            lax.all_to_all(shipped[:, None], "dp", split_axis=0, concat_axis=0, tiled=True),
            lax.all_to_all(shipped_meta[:, None], "dp", split_axis=0, concat_axis=0, tiled=True),
            pool_keys,
            pool_values,
            score_scale,
        )
        back_mixed = lax.all_to_all(mixed_part, "dp", split_axis=0, concat_axis=0, tiled=True)
        back_logs = lax.all_to_all(log_part, "dp", split_axis=0, concat_axis=0, tiled=True)
        outputs.append(
            jnp.take(back_mixed[:, 0], targets, axis=0).reshape(
                group_requests, leaf_len, local_heads, head_dim
            )
        )
        log_totals.append(jnp.take(back_logs[:, 0], targets, axis=0))
    attended = (
        merge_parts(outputs, log_totals)
        .astype(jnp.bfloat16)
        .reshape(group_requests, leaf_len, local_width)
    )
    residual_mid = residual + lax.psum_scatter(
        jnp.einsum("alk,kd->ald", attended, w_out, preferred_element_type=jnp.float32).astype(
            jnp.bfloat16
        ),
        "tensor",
        scatter_dimension=0,
        tiled=True,
    ).astype(jnp.float32)
    normed_mlp = rms_scaled(residual_mid, mlp_gain).astype(jnp.bfloat16)
    mlp_rows = lax.all_gather(normed_mlp, "tensor", axis=0, tiled=True)
    gate_up = jnp.einsum(
        "ald,df->alf",
        mlp_rows,
        shared_in.reshape(model_width, -1),
        preferred_element_type=jnp.float32,
    )
    half_width = gate_up.shape[-1] // 2
    shared_hidden = (jax.nn.silu(gate_up[..., :half_width]) * gate_up[..., half_width:]).astype(
        jnp.bfloat16
    )
    shared_part = jnp.einsum(
        "alf,fd->ald", shared_hidden, shared_out, preferred_element_type=jnp.float32
    )
    top_count = expert_ids.shape[2]
    experts_all = expert_in.shape[0] * groups
    block_rows = group_requests * leaf_len
    assignments = block_rows * top_count
    capacity = tensors * max(1, assignments * 4 // (experts_all * 3 * tensors))
    route_ids = expert_ids.reshape(assignments)
    chosen = (route_ids[:, None] == jnp.arange(experts_all)[None, :]).astype(jnp.int32)
    before = jnp.cumsum(chosen, axis=0) - chosen
    slot_of = jnp.sum(before * chosen, axis=1)
    flat_slot = route_ids * capacity + slot_of
    source_row = jnp.arange(assignments) // top_count
    filler = jnp.zeros((experts_all * capacity,), jnp.int32).at[flat_slot].set(source_row + 1)
    flat_rows = mlp_rows.reshape(block_rows, model_width)
    send_rows = jnp.where(
        (filler > 0)[:, None],
        jnp.take(flat_rows, jnp.maximum(filler - 1, 0), axis=0),
        jnp.zeros((), jnp.bfloat16),
    )
    send_rows = send_rows.reshape(experts_all, capacity, model_width)
    weight_in = expert_in.reshape(expert_in.shape[0], model_width, -1)
    gate_flat = gate_weights.reshape(assignments, 1)
    returned = lax.all_to_all(
        expert_partial(
            lax.all_to_all(send_rows, "dp", split_axis=0, concat_axis=0, tiled=True),
            weight_in,
            expert_out,
            groups,
        ),
        "dp",
        split_axis=0,
        concat_axis=0,
        tiled=True,
    )
    picked = jnp.take(returned.reshape(experts_all * capacity, model_width), flat_slot, axis=0)
    routed = jnp.sum((picked * gate_flat).reshape(block_rows, top_count, model_width), axis=1)
    layer_term = shared_part + routed.reshape(group_requests, leaf_len, model_width)
    first_request = lax.axis_index("tensor") * shard_requests
    own_block = (
        lax.dynamic_slice_in_dim(layer_term, first_request, shard_requests, 0) + residual_mid
    )
    layer_term = lax.dynamic_update_slice_in_dim(layer_term, own_block, first_request, 0)
    mixed_rows = lax.psum_scatter(
        layer_term.astype(jnp.bfloat16), "tensor", scatter_dimension=1, tiled=True
    )
    targets_back = request_of // group_requests
    places = request_of % group_requests
    sending = targets_back[:, None] == owner_ids[None, :]
    outgoing = jnp.einsum(
        "ag,ald->gld", sending.astype(jnp.bfloat16), mixed_rows, preferred_element_type=jnp.float32
    ).astype(jnp.bfloat16)
    slot_tags = jnp.sum(sending.astype(jnp.int32) * (places + 1)[:, None], axis=0)
    arrived_rows, arrived_tags = (
        lax.all_to_all(outgoing, "dp", split_axis=0, concat_axis=0, tiled=True),
        lax.all_to_all(slot_tags, "dp", split_axis=0, concat_axis=0, tiled=True),
    )
    settle = arrived_tags[None, :] == jnp.arange(group_requests)[:, None] + 1
    return jnp.einsum(
        "ag,gld->ald", settle.astype(jnp.bfloat16), arrived_rows, preferred_element_type=jnp.float32
    ).astype(jnp.bfloat16)


def solution(mesh):
    in_specs = (
        P(("dp", "tensor"), None, None),
        P(),
        P(None, "tensor"),
        P(None, "tensor"),
        P(None, "tensor"),
        P("tensor", None),
        P(None, "dp", "tensor"),
        P("dp", None),
        P("dp", None),
        P("dp", None),
        P(),
        P(None, None, "tensor"),
        P("tensor", None),
        P("dp", None, None, "tensor"),
        P("dp", "tensor", None),
        P("dp", None, None),
        P("dp", None, None),
        P("dp"),
    )
    out_specs = P("dp", "tensor", None)
    return jax.shard_map(
        on_device, mesh=mesh, in_specs=in_specs, out_specs=out_specs, check_vma=False
    )
```

profile of v0, /device:TPU:2, one launch (start us, length us, event | category | flops | bytes accessed | tf_op | source)
XLA Modules:
  0.0 641.7 jit_solution(15907566742419996335)
XLA Ops:
  10.3 14.3 %all-to-all-start.7 = ((s32[32,1,2]{2,1,0:T(1,128)}), s32[32,1,2]{2,1,0:T(1,128)}, u32[]{:S(2)}, u32[]{:S(2)}) async-start(s32[32,1,2]{2,1,0:T(1,128)} %copy.175), calls=%async_computation.7 | async-start | bytes 32768 | tf_op jit(solution)/shard_map/all_to_all | solution.py:191
  29.3 14.9 %all_gather.6 = bf16[16,8,2048]{2,1,0:T(8,128)(2,1)S(1)} all-gather(bf16[2,8,2048]{2,1,0:T(8,128)(2,1)S(1)} %fusion.65), channel_id=1, replica_groups=mesh['dp'=32,'tensor'=8] {'tensor'}, dimensions={0}, use_global_device_ids=true | all-gather | bytes 589824 | tf_op jit(solution)/shard_map/all_gather | solution.py:138
  60.1 2.0 copy.217
  64.1 12.2 %all-to-all-start.4 = ((s32[32,1,2]{2,1,0:T(1,128)}), s32[32,1,2]{2,1,0:T(1,128)S(1)}, u32[]{:S(2)}, u32[]{:S(2)}) async-start(s32[32,1,2]{2,1,0:T(1,128)} %copy.169), calls=%async_computation.4 | async-start | bytes 32768 | tf_op jit(solution)/shard_map/all_to_all | solution.py:191
  76.3 2.1 slice_reduce_fusion.1
  78.6 8.7 %all-to-all-done.4 = s32[32,1,2]{2,1,0:T(1,128)S(1)} async-done(((s32[32,1,2]{2,1,0:T(1,128)}), s32[32,1,2]{2,1,0:T(1,128)S(1)}, u32[]{:S(2)}, u32[]{:S(2)}) %all-to-all-start.4) | async-done | bytes 288 | tf_op jit(solution)/shard_map/all_to_all | solution.py:191
  87.2 4.8 all-to-all-start.1
  96.0 7.2 %all-to-all-done.1 = s32[32,1,2]{2,1,0:T(1,128)S(1)} async-done(((s32[32,1,2]{2,1,0:T(1,128)}), s32[32,1,2]{2,1,0:T(1,128)S(1)}, u32[]{:S(2)}, u32[]{:S(2)}) %all-to-all-start.1) | async-done | bytes 288 | tf_op jit(solution)/shard_map/all_to_all | solution.py:191
  103.7 5.1 all-to-all-start.8
  108.9 2.7 slice_reduce_fusion.5
  120.9 10.6 %all-to-all-start.5 = ((bf16[32,1,8,256]{3,2,1,0:T(8,128)(2,1)}), bf16[32,1,8,256]{3,2,1,0:T(8,128)(2,1)}, u32[]{:S(2)}, u32[]{:S(2)}) async-start(bf16[32,1,8,256]{3,2,1,0:T(8,128)(2,1)} %copy.171), calls=%async_computation.5 | async-start | bytes 262144 | tf_op jit(solution)/shard_map/all_to_all | solution.py:190
  138.1 4.9 all-to-all-done.5
  143.0 8.0 %all-to-all-start.2 = ((bf16[32,1,8,256]{3,2,1,0:T(8,128)(2,1)}), bf16[32,1,8,256]{3,2,1,0:T(8,128)(2,1)}, u32[]{:S(2)}, u32[]{:S(2)}) async-start(bf16[32,1,8,256]{3,2,1,0:T(8,128)(2,1)} %copy.164), calls=%async_computation.2 | async-start | bytes 262144 | tf_op jit(solution)/shard_map/all_to_all | solution.py:190
  158.3 4.0 all-to-all-done.2
  162.3 8.2 %all-to-all-start.9 = ((f32[32,1,8,2]{2,3,1,0:T(2,128)}), f32[32,1,8,2]{2,3,1,0:T(2,128)}, u32[]{:S(2)}, u32[]{:S(2)}) async-start(f32[32,1,8,2]{2,3,1,0:T(2,128)} %copy.180), calls=%async_computation.9 | async-start | bytes 65536 | tf_op jit(solution)/shard_map/all_to_all | solution.py:197
  176.5 5.1 all-to-all-done.9
  181.6 7.2 %all-to-all-start.6 = ((f32[32,1,8,2]{2,3,1,0:T(2,128)}), f32[32,1,8,2]{2,3,1,0:T(2,128)S(1)}, u32[]{:S(2)}, u32[]{:S(2)}) async-start(f32[32,1,8,2]{2,3,1,0:T(2,128)} %copy.174), calls=%async_computation.6 | async-start | bytes 65536 | tf_op jit(solution)/shard_map/all_to_all | solution.py:197
  189.4 10.3 %all-to-all-done.6 = f32[32,1,8,2]{2,3,1,0:T(2,128)S(1)} async-done(((f32[32,1,8,2]{2,3,1,0:T(2,128)}), f32[32,1,8,2]{2,3,1,0:T(2,128)S(1)}, u32[]{:S(2)}, u32[]{:S(2)}) %all-to-all-start.6) | async-done | bytes 2080 | tf_op jit(solution)/shard_map/all_to_all | solution.py:197
  199.7 5.0 all-to-all-start.3
  204.7 2.3 fusion.17
  209.8 6.0 all-to-all-done.3
  215.7 6.4 all-to-all-start.12
  226.6 2.2 fusion.31
  228.8 2.3 fusion.18
  234.3 10.2 %all-to-all-start.11 = ((f32[32,1,8,256]{3,2,1,0:T(8,128)}), f32[32,1,8,256]{3,2,1,0:T(8,128)S(1)}, u32[]{:S(2)}, u32[]{:S(2)}) async-start(f32[32,1,8,256]{3,2,1,0:T(8,128)} %bitcast.52), calls=%async_computation.11 | async-start | bytes 524288 | tf_op jit(solution)/shard_map/all_to_all | solution.py:196
  245.1 2.2 fusion.19
  251.3 5.3 all-to-all-done.11
  256.6 6.9 %all-to-all-start.10 = ((f32[32,1,8,256]{3,2,1,0:T(8,128)}), f32[32,1,8,256]{3,2,1,0:T(8,128)S(1)}, u32[]{:S(2)}, u32[]{:S(2)}) async-start(f32[32,1,8,256]{3,2,1,0:T(8,128)} %bitcast.47), calls=%async_computation.10 | async-start | bytes 524288 | tf_op jit(solution)/shard_map/all_to_all | solution.py:196
  266.0 2.3 gather_fusion.7
  269.6 6.1 all-to-all-done.10
  276.4 3.0 convolution_convert_fusion
  281.8 3.4 scatter_custom_fusion
  285.3 25.4 %reduce-scatter.3.cloned.1.call-done = bf16[2,8,2048]{2,1,0:T(8,128)(2,1)} async-done(((bf16[16,8,2048]{2,1,0:T(8,128)(2,1)}), bf16[2,8,2048]{2,1,0:T(8,128)(2,1)}) %reduce-scatter.3.cloned.1.call-update) | async-done | bytes 65552 | tf_op jit(solution)/shard_map/reduce_scatter | solution.py:209
  312.6 15.0 %all_gather.7 = bf16[16,8,2048]{2,1,0:T(8,128)(2,1)S(1)} all-gather(bf16[2,8,2048]{2,1,0:T(8,128)(2,1)S(1)} %multiply_convert_fusion), channel_id=1, replica_groups=mesh['dp'=32,'tensor'=8] {'tensor'}, dimensions={0}, use_global_device_ids=true | all-gather | bytes 589824 | tf_op jit(solution)/shard_map/all_gather | solution.py:218
  327.6 6.0 gather_fusion
  333.7 2.6 select_select_fusion
  336.2 108.5 %all_to_all.84 = bf16[64,16,2048]{2,1,0:T(8,128)(2,1)S(1)} all-to-all(bf16[64,16,2048]{2,1,0:T(8,128)(2,1)S(1)} %select_select_fusion), channel_id=1, replica_groups=mesh['dp'=32,'tensor'=8] {'dp'}, dimensions={0} | all-to-all | bytes 8388608 | tf_op jit(solution)/shard_map/all_to_all | solution.py:255
  444.7 2.3 fusion.7
  448.4 2.3 copy.200
  450.7 5.9 all-to-all-start.14
  458.2 95.3 %all-to-all-done.14 = bf16[64,16,2048]{2,1,0:T(8,128)(2,1)} async-done(((bf16[64,16,2048]{2,1,0:T(8,128)(2,1)}), bf16[64,16,2048]{2,1,0:T(8,128)(2,1)}, u32[]{:S(2)}, u32[]{:S(2)}) %all-to-all-start.14) | async-done | bytes 4194336 | tf_op jit(solution)/shard_map/all_to_all | solution.py:253
  553.5 9.8 %gather_fusion.1 = bf16[768,2048]{1,0:T(8,128)(2,1)} fusion(bf16[1024,2048]{1,0:T(8,128)(2,1)} %bitcast.77, s32[1024]{0:T(1024)S(1)} %pad_clamp_fusion), kind=kCustom, calls=%fused_computation.7 | custom fusion | bytes 6294528 | tf_op jit(solution)/shard_map/jit(_take)/gather | solution.py:265
  563.3 6.2 gather.21
  569.6 6.0 multiply_reduce_fusion
  578.5 3.6 all-to-all-start
  582.1 27.2 %reduce-scatter.5.cloned.1.call-done = bf16[16,1,2048]{2,0,1:T(8,128)(2,1)} async-done(((bf16[16,8,2048]{2,0,1:T(8,128)(2,1)}), bf16[16,1,2048]{2,0,1:T(8,128)(2,1)}) %reduce-scatter.5.cloned.1.call-update) | async-done | bytes 65552 | tf_op jit(solution)/shard_map/reduce_scatter | solution.py:273
  612.4 9.9 %all-to-all-start.15 = ((bf16[32,2,1024]{2,1,0:T(2,128)(2,1)}), bf16[32,2,1024]{2,1,0:T(2,128)(2,1)S(1)}, u32[]{:S(2)}, u32[]{:S(2)}) async-start(bf16[32,2,1024]{2,1,0:T(2,128)(2,1)} %reshape.826), calls=%async_computation.17 | async-start | bytes 262144 | tf_op jit(solution)/shard_map/all_to_all | solution.py:284
  623.0 10.7 %all-to-all-done.15 = bf16[32,2,1024]{2,1,0:T(2,128)(2,1)S(1)} async-done(((bf16[32,2,1024]{2,1,0:T(2,128)(2,1)}), bf16[32,2,1024]{2,1,0:T(2,128)(2,1)S(1)}, u32[]{:S(2)}, u32[]{:S(2)}) %all-to-all-start.15) | async-done | bytes 131104 | tf_op jit(solution)/shard_map/all_to_all | solution.py:284
  (253 shorter events, 94.6 us)
Async XLA Ops:
  6.5 438.2 %copy-start = (bf16[2,2048,2,176]{1,3,2,0:T(8,128)(2,1)S(1)}, bf16[2,2048,2,176]{1,3,2,0:T(8,128)(2,1)}, u32[]{:S(2)}) copy-start(bf16[2,2048,2,176]{1,3,2,0:T(8,128)(2,1)} %param.35) | copy-start | bytes 8650756
  10.3 53.9 %all-to-all-start.7 = ((s32[32,1,2]{2,1,0:T(1,128)}), s32[32,1,2]{2,1,0:T(1,128)}, u32[]{:S(2)}, u32[]{:S(2)}) async-start(s32[32,1,2]{2,1,0:T(1,128)} %copy.175), calls=%async_computation.7 | async-start | bytes 32768 | tf_op jit(solution)/shard_map/all_to_all | solution.py:191
  27.3 18.5 %copy-start.11 = (bf16[2048,256]{1,0:T(8,128)(2,1)S(1)}, bf16[2048,256]{1,0:T(8,128)(2,1)}, u32[]{:S(2)}) copy-start(bf16[2048,256]{1,0:T(8,128)(2,1)} %param.24) | copy-start | bytes 3145732
  45.7 3.2 copy-start.24
  45.8 3.8 copy-start.48
  45.8 4.1 copy-start.12
  46.4 4.5 copy-start.43
  46.4 5.1 copy-start.46
  46.4 5.1 copy-start.47
  46.4 5.7 copy-start.26
  46.5 5.7 copy-start.42
  49.9 3.6 copy-start.25
  64.1 23.1 %all-to-all-start.4 = ((s32[32,1,2]{2,1,0:T(1,128)}), s32[32,1,2]{2,1,0:T(1,128)S(1)}, u32[]{:S(2)}, u32[]{:S(2)}) async-start(s32[32,1,2]{2,1,0:T(1,128)} %copy.169), calls=%async_computation.4 | async-start | bytes 32768 | tf_op jit(solution)/shard_map/all_to_all | solution.py:191
  87.2 15.9 %all-to-all-start.1 = ((s32[32,1,2]{2,1,0:T(1,128)}), s32[32,1,2]{2,1,0:T(1,128)S(1)}, u32[]{:S(2)}, u32[]{:S(2)}) async-start(s32[32,1,2]{2,1,0:T(1,128)} %copy.162), calls=%async_computation.1 | async-start | bytes 32768 | tf_op jit(solution)/shard_map/all_to_all | solution.py:191
  103.7 16.6 %all-to-all-start.8 = ((bf16[32,1,8,256]{3,2,1,0:T(8,128)(2,1)}), bf16[32,1,8,256]{3,2,1,0:T(8,128)(2,1)S(1)}, u32[]{:S(2)}, u32[]{:S(2)}) async-start(bf16[32,1,8,256]{3,2,1,0:T(8,128)(2,1)} %copy.177), calls=%async_computation.8 | async-start | bytes 262144 | tf_op jit(solution)/shard_map/all_to_all | solution.py:190
  120.9 22.1 %all-to-all-start.5 = ((bf16[32,1,8,256]{3,2,1,0:T(8,128)(2,1)}), bf16[32,1,8,256]{3,2,1,0:T(8,128)(2,1)}, u32[]{:S(2)}, u32[]{:S(2)}) async-start(bf16[32,1,8,256]{3,2,1,0:T(8,128)(2,1)} %copy.171), calls=%async_computation.5 | async-start | bytes 262144 | tf_op jit(solution)/shard_map/all_to_all | solution.py:190
  132.5 3.0 copy-start.8
  134.8 8.2 %copy-start.39 = (f32[256,2]{0,1:T(2,128)}, f32[256,2]{0,1:T(2,128)S(1)}, u32[]{:S(2)}) copy-start(f32[256,2]{0,1:T(2,128)S(1)} %is-finite_select_fusion.5) | copy-start | bytes 6148
  143.0 19.3 %all-to-all-start.2 = ((bf16[32,1,8,256]{3,2,1,0:T(8,128)(2,1)}), bf16[32,1,8,256]{3,2,1,0:T(8,128)(2,1)}, u32[]{:S(2)}, u32[]{:S(2)}) async-start(bf16[32,1,8,256]{3,2,1,0:T(8,128)(2,1)} %copy.164), calls=%async_computation.2 | async-start | bytes 262144 | tf_op jit(solution)/shard_map/all_to_all | solution.py:190
  152.0 3.0 copy-start.5
  152.0 3.6 copy-start.21
  152.0 3.6 copy-start.22
  162.3 19.3 %all-to-all-start.9 = ((f32[32,1,8,2]{2,3,1,0:T(2,128)}), f32[32,1,8,2]{2,3,1,0:T(2,128)}, u32[]{:S(2)}, u32[]{:S(2)}) async-start(f32[32,1,8,2]{2,3,1,0:T(2,128)} %copy.180), calls=%async_computation.9 | async-start | bytes 65536 | tf_op jit(solution)/shard_map/all_to_all | solution.py:197
  181.6 18.1 %all-to-all-start.6 = ((f32[32,1,8,2]{2,3,1,0:T(2,128)}), f32[32,1,8,2]{2,3,1,0:T(2,128)S(1)}, u32[]{:S(2)}, u32[]{:S(2)}) async-start(f32[32,1,8,2]{2,3,1,0:T(2,128)} %copy.174), calls=%async_computation.6 | async-start | bytes 65536 | tf_op jit(solution)/shard_map/all_to_all | solution.py:197
  199.7 16.0 %all-to-all-start.3 = ((f32[32,1,8,2]{2,3,1,0:T(2,128)}), f32[32,1,8,2]{2,3,1,0:T(2,128)S(1)}, u32[]{:S(2)}, u32[]{:S(2)}) async-start(f32[32,1,8,2]{2,3,1,0:T(2,128)} %copy.168), calls=%async_computation.3 | async-start | bytes 65536 | tf_op jit(solution)/shard_map/all_to_all | solution.py:197
  204.7 17.5 %copy-start.45 = (s32[16]{0:T(128)S(1)}, s32[16]{0:T(128)}, u32[]{:S(2)}) copy-start(s32[16]{0:T(128)} %get-tuple-element.16) | copy-start | bytes 196
  215.7 18.5 %all-to-all-start.12 = ((f32[32,1,8,256]{3,2,1,0:T(8,128)}), f32[32,1,8,256]{3,2,1,0:T(8,128)}, u32[]{:S(2)}, u32[]{:S(2)}) async-start(f32[32,1,8,256]{3,2,1,0:T(8,128)} %bitcast.295), calls=%async_computation.12 | async-start | bytes 524288 | tf_op jit(solution)/shard_map/all_to_all | solution.py:196
  228.8 15.7 %copy-start.18 = (f32[16,2,8]{2,1,0:T(2,128)S(1)}, f32[16,2,8]{2,1,0:T(2,128)}, u32[]{:S(2)}) copy-start(f32[16,2,8]{2,1,0:T(2,128)} %fusion.79) | copy-start | bytes 3076
  228.8 16.3 %copy-start.7 = (pred[256,896]{1,0:T(8,128)(4,1)S(1)}, pred[256,896]{1,0:T(8,128)(4,1)}, u32[]{:S(2)}) copy-start(pred[256,896]{1,0:T(8,128)(4,1)} %fusion.50) | copy-start | bytes 688132
  228.8 16.3 %copy-start.41 = (f32[256,2]{0,1:T(2,128)S(1)}, f32[256,2]{0,1:T(2,128)}, u32[]{:S(2)}) copy-start(f32[256,2]{0,1:T(2,128)} %copy-done.40) | copy-start | bytes 6148
  228.8 16.3 %copy-start.44 = (f32[256,2]{0,1:T(2,128)S(1)}, f32[256,2]{0,1:T(2,128)}, u32[]{:S(2)}) copy-start(f32[256,2]{0,1:T(2,128)} %get-tuple-element.49) | copy-start | bytes 6148
  234.3 22.3 %all-to-all-start.11 = ((f32[32,1,8,256]{3,2,1,0:T(8,128)}), f32[32,1,8,256]{3,2,1,0:T(8,128)S(1)}, u32[]{:S(2)}, u32[]{:S(2)}) async-start(f32[32,1,8,256]{3,2,1,0:T(8,128)} %bitcast.52), calls=%async_computation.11 | async-start | bytes 524288 | tf_op jit(solution)/shard_map/all_to_all | solution.py:196
  256.6 19.1 %all-to-all-start.10 = ((f32[32,1,8,256]{3,2,1,0:T(8,128)}), f32[32,1,8,256]{3,2,1,0:T(8,128)S(1)}, u32[]{:S(2)}, u32[]{:S(2)}) async-start(f32[32,1,8,256]{3,2,1,0:T(8,128)} %bitcast.47), calls=%async_computation.10 | async-start | bytes 524288 | tf_op jit(solution)/shard_map/all_to_all | solution.py:196
  263.5 47.2 %reduce-scatter.3.cloned.1.call-start = ((), (), s32[]{:S(2)}) async-start(), calls=%async_computation.18 | async-start | bytes 589824 | tf_op jit(solution)/shard_map/reduce_scatter | solution.py:209
  276.4 3.1 copy-start.35
  276.4 5.2 copy-start.34
  276.4 5.3 copy-start.36
  276.4 34.4 %copy-start.9 = (bf16[2,8,2048]{2,1,0:T(8,128)(2,1)S(1)}, bf16[2,8,2048]{2,1,0:T(8,128)(2,1)}, u32[]{:S(2)}) copy-start(bf16[2,8,2048]{2,1,0:T(8,128)(2,1)} %param.22) | copy-start | bytes 196612
  276.4 35.3 %copy-start.37 = (f32[2048]{0:T(1024)S(1)}, f32[2048]{0:T(1024)}, u32[]{:S(2)}) copy-start(f32[2048]{0:T(1024)} %param.32) | copy-start | bytes 24580
  450.7 6.2 copy-start.17
  450.7 6.5 %copy-start.27 = (f32[16,8,6]{0,1,2:T(8,128)S(1)}, f32[16,8,6]{0,1,2:T(8,128)}, u32[]{:S(2)}) copy-start(f32[16,8,6]{0,1,2:T(8,128)} %param.38) | copy-start | bytes 9220
  450.7 6.9 %copy-start.10 = (bf16[2048,2,176]{0,2,1:T(8,128)(2,1)S(1)}, bf16[2048,2,176]{0,2,1:T(8,128)(2,1)}, u32[]{:S(2)}) copy-start(bf16[2048,2,176]{0,2,1:T(8,128)(2,1)} %param.33) | copy-start | bytes 4325380
  450.7 102.8 %all-to-all-start.14 = ((bf16[64,16,2048]{2,1,0:T(8,128)(2,1)}), bf16[64,16,2048]{2,1,0:T(8,128)(2,1)}, u32[]{:S(2)}, u32[]{:S(2)}) async-start(bf16[64,16,2048]{2,1,0:T(8,128)(2,1)} %bitcast.289), calls=%async_computation.15 | async-start | bytes 8388608 | tf_op jit(solution)/shard_map/all_to_all | solution.py:253
  456.6 152.7 %reduce-scatter.5.cloned.1.call-start = ((), (), s32[]{:S(2)}) async-start(), calls=%async_computation.19 | async-start | bytes 589824 | tf_op jit(solution)/shard_map/reduce_scatter | solution.py:273
  569.6 6.0 copy-start.13
  576.5 58.2 %copy-start.1 = (bf16[2,2048,2,176]{1,3,2,0:T(8,128)(2,1)S(1)}, bf16[2,2048,2,176]{1,3,2,0:T(8,128)(2,1)}, u32[]{:S(2)}) copy-start(bf16[2,2048,2,176]{1,3,2,0:T(8,128)(2,1)} %param.35) | copy-start | bytes 8650756
  578.5 33.9 %all-to-all-start = ((s32[32,1,1]{2,1,0:T(1,128)}), s32[32,1,1]{2,1,0:T(1,128)S(1)}, u32[]{:S(2)}, u32[]{:S(2)}) async-start(s32[32,1,1]{2,1,0:T(1,128)} %copy.161), calls=%async_computation | async-start | bytes 32768 | tf_op jit(solution)/shard_map/all_to_all | solution.py:285
  612.4 21.3 %all-to-all-start.15 = ((bf16[32,2,1024]{2,1,0:T(2,128)(2,1)}), bf16[32,2,1024]{2,1,0:T(2,128)(2,1)S(1)}, u32[]{:S(2)}, u32[]{:S(2)}) async-start(bf16[32,2,1024]{2,1,0:T(2,128)(2,1)} %reshape.826), calls=%async_computation.17 | async-start | bytes 262144 | tf_op jit(solution)/shard_map/all_to_all | solution.py:284
  (20 other events, 26.4 us)
Sparse Core Ops, SparseCore 0:
  279.5 31.1 reduce-scatter.2
  577.8 31.5 reduce-scatter.4
where the time goes:
time: 652 us; the launch traced here: 642 us
  waiting for transfers between devices  220 us (34%)
  blocking collectives  138 us (21%)
  starting transfers between devices  119 us (18%)
  local copies, waits for them, and re-layouts  86.5 us (13%)
  other arithmetic  35.7 us (5%)
  matrix products  27.9 us (4%)
  between operations  14.6 us (2%)
    all_to_all x1, blocking collectives, on_device(): lax.all_to_all(send_rows, 'dp', split_axis=0, concat_axis=0, tiled=True)  108 us
    all_to_all x1, waiting for transfers between devices, on_device(): lax.all_to_all(expert_partial(lax.all_to_all(send_rows, 'dp', split_axis=...  95.3 us
    all_to_all x3, starting transfers between devices, on_device(): lax.all_to_all(shipped_meta[:, None], 'dp', split_axis=0, concat_axis=0,...  31.3 us
    reduce_scatter x1, waiting for transfers between devices, on_device(): lax.psum_scatter(layer_term.astype(jnp.bfloat16), 'tensor', scatter_dimen...  27.2 us
    reduce_scatter x1, waiting for transfers between devices, on_device(): lax.psum_scatter(jnp.einsum('alk,kd->ald', attended, w_out, preferred_ele...  25.4 us
    all_to_all x3, starting transfers between devices, on_device(): lax.all_to_all(shipped[:, None], 'dp', split_axis=0, concat_axis=0, tiled...  23.7 us
    all_to_all x3, starting transfers between devices, on_device(): lax.all_to_all(mixed_part, 'dp', split_axis=0, concat_axis=0, tiled=True)  23.5 us
    all_to_all x3, waiting for transfers between devices, on_device(): lax.all_to_all(log_part, 'dp', split_axis=0, concat_axis=0, tiled=True)  21.3 us
  transfers between devices with their start and end apart: 17, of which 15 were waited for; matrix products, arithmetic and copies ran while one was open for 15% of the time, Pallas kernels for 0%

commit v1 on v0

v1 whole, which is shorter than its diff:
```python
import jax
import jax.numpy as jnp
from jax import lax
from jax.experimental import pallas as pl
from jax.experimental.pallas import tpu as pltpu
from jax.sharding import PartitionSpec as P

HEAD_DIM = 128
EPS = 1e-06
ROPE_BASE = 10000.0
MESH = pl.DeviceIdType.MESH
BF = jnp.bfloat16
F32 = jnp.float32
NEG = -1e30


def nt_dot(a, b):
    return lax.dot_general(a, b, (((1,), (1,)), ((), ())), preferred_element_type=F32)


def nn_dot(a, b):
    return jnp.dot(a, b, preferred_element_type=F32)


def rms_rows(values, gain):
    mean_square = jnp.mean(values * values, axis=-1, keepdims=True)
    return (values * lax.rsqrt(mean_square + EPS) * gain).astype(BF)


def iota(shape, dim):
    return lax.broadcasted_iota(jnp.int32, shape, dim)


class Place:
    def __init__(self):
        self.groups = lax.axis_size("dp")
        self.me = lax.axis_index("dp")
        self.t = lax.axis_index("tensor")
        self.chip = self.t // 2
        self.core = lax.rem(self.t, 2)
        self.sib = self.chip * 2 + (1 - self.core)

    def ahead(self, k):
        return lax.rem(self.me + k, self.groups)

    def behind(self, k):
        return lax.rem(self.me + self.groups - k, self.groups)

    def lane(self, k):
        return lax.rem(self.chip + k, 4) * 2 + self.core


def to_group(src, dst, send, recv, group):
    return pltpu.make_async_remote_copy(
        src, dst, send, recv, device_id={"dp": group}, device_id_type=MESH
    )


def to_lane(src, dst, send, recv, lane):
    return pltpu.make_async_remote_copy(
        src, dst, send, recv, device_id={"tensor": lane}, device_id_type=MESH
    )


def announce(p):
    barrier = pltpu.get_barrier_semaphore()

    def signal(k, carry):
        pl.semaphore_signal(barrier, inc=1, device_id={"dp": p.ahead(k)}, device_id_type=MESH)
        return carry

    pl.semaphore_signal(barrier, inc=1, device_id={"tensor": p.sib}, device_id_type=MESH)
    for k in range(1, 4):
        pl.semaphore_signal(barrier, inc=1, device_id={"tensor": p.lane(k)}, device_id_type=MESH)
    lax.fori_loop(1, p.groups, signal, 0)


def await_all(p):
    pl.semaphore_wait(pltpu.get_barrier_semaphore(), p.groups - 1 + 4)


def gather_rows(p, buf, sems, between=None):
    send, recv = sems
    direct = []
    for k in range(1, 4):
        copy = to_lane(buf.at[p.t], buf.at[p.t], send.at[k], recv.at[k], p.lane(k))
        copy.start()
        direct.append(copy)
    passed = [to_lane(buf.at[p.t], buf.at[p.t], send.at[0], recv.at[0], p.sib)]
    passed[0].start()
    if between is not None:
        between()
    for k in range(1, 4):
        direct[k - 1].wait_recv()
        source = p.lane(4 - k)
        copy = to_lane(buf.at[source], buf.at[source], send.at[3 + k], recv.at[3 + k], p.sib)
        copy.start()
        passed.append(copy)
    for copy in direct:
        copy.wait_send()
    for copy in passed:
        copy.wait()


def scatter_sum(p, part, sib_send, sib_recv, rs_send, rs_recv, sems):
    send, recv = sems
    for c in range(4):
        sib_send[c] = part[c * 2 + (1 - p.core)].astype(BF)
    swap = to_lane(sib_send, sib_recv, send.at[0], recv.at[0], p.sib)
    swap.start()
    swap.wait_recv()
    copies = []
    for k in range(1, 4):
        there = lax.rem(p.chip + k, 4)
        rs_send[k - 1] = (part[there * 2 + p.core] + sib_recv[there].astype(F32)).astype(BF)
        copy = to_lane(rs_send.at[k - 1], rs_recv.at[k - 1], send.at[k], recv.at[k], p.lane(k))
        copy.start()
        copies.append(copy)
    total = part[p.t] + sib_recv[p.chip].astype(F32)
    for k in range(1, 4):
        copies[k - 1].wait_recv()
        total = total + rs_recv[k - 1].astype(F32)
    swap.wait_send()
    for copy in copies:
        copy.wait_send()
    return total


def attention_kernel(
    leaf, gain1, gain2, table, wq_hbm, wk_hbm, wv_hbm, wo_hbm, kv_hbm, ein_hbm, eout_hbm,
    res_out, mlp_out, ein_swap, eout_swap,
    wq, wk, wv, wo, kv, xg, qs, qr, bs, br, part, sib_send, sib_recv, rs_send, rs_recv,
    load_sem, swap_send, swap_recv, g1_send, g1_recv, g2_send, g2_recv,
    q_send, q_recv, b_send, b_recv, r_send, r_recv,
):
    p = Place()
    groups = p.groups
    lanes, shard_rows, width = xg.shape
    rows = lanes * shard_rows
    heads = wq.shape[1] // HEAD_DIM
    slot_rows = qs.shape[1]
    leaf_len = slot_rows // 2
    keys = kv.shape[1]
    scale = HEAD_DIM**-0.5

    loads = []
    for j, (src, dst) in enumerate(
        ((wq_hbm, wq), (wk_hbm, wk), (wv_hbm, wv), (wo_hbm, wo), (kv_hbm, kv))
    ):
        copy = pltpu.make_async_copy(src, dst, load_sem.at[j])
        copy.start()
        loads.append(copy)
    announce(p)
    residual = leaf[...].astype(F32)
    xg[p.t] = rms_rows(residual, gain1[...])
    await_all(p)
    other = 1 - p.core
    swaps = [
        to_lane(ein_hbm.at[other], ein_swap, swap_send.at[0], swap_recv.at[0], p.sib),
        to_lane(eout_hbm.at[other], eout_swap, swap_send.at[1], swap_recv.at[1], p.sib),
    ]
    gather_rows(p, xg, (g1_send, g1_recv))
    for copy in swaps:
        copy.start()

    cols = jnp.transpose(table[...], (1, 0))
    lane = iota((rows, HEAD_DIM), 1)
    half = HEAD_DIM // 2
    frequency = jnp.exp(
        (-2.0 / HEAD_DIM * jnp.log(ROPE_BASE)) * lax.rem(lane, half).astype(F32)
    )
    angles = cols[:, 9:10] * frequency
    cosine = jnp.cos(angles)
    sine = jnp.where(lane < half, -1.0, 1.0) * jnp.sin(angles)

    def rotated(values):
        pieces = []
        for h in range(heads):
            one = values[:, h * HEAD_DIM : (h + 1) * HEAD_DIM]
            pieces.append(one * cosine + pltpu.roll(one, half, 1) * sine)
        return jnp.concatenate(pieces, axis=1).astype(BF)

    x = xg[...].reshape(rows, width)
    loads[0].wait()
    queries = rotated(nn_dot(x, wq[...]))

    stacked = []
    places = []
    slot_index = iota((groups * slot_rows, rows), 0).astype(F32)
    for level in range(3):
        start = cols[:, 3 + level : 4 + level]
        count = cols[:, 6 + level : 7 + level]
        start_hi = jnp.floor(start * (1.0 / 32.0))
        count_hi = jnp.floor(count * (1.0 / 32.0))
        meta = jnp.where(
            lane == 0,
            start_hi,
            jnp.where(
                lane == 1,
                start - 32.0 * start_hi,
                jnp.where(lane == 2, count_hi, jnp.where(lane == 3, count - 32.0 * count_hi, 0.0)),
            ),
        )
        stacked.append(jnp.concatenate([queries, meta.astype(BF)], axis=1))
        places.append((slot_index == table[level : level + 1, :]).astype(F32).astype(BF))
    packed = nn_dot(jnp.concatenate(places, axis=1), jnp.concatenate(stacked, axis=0))
    qs[...] = packed.astype(BF).reshape(qs.shape)

    def q_copy(k):
        return to_group(qs.at[k], qr.at[k], q_send.at[k], q_recv.at[k], p.ahead(k))

    def b_copy(k):
        return to_group(bs.at[k], br.at[k], b_send.at[k], b_recv.at[k], p.behind(k))

    def start_q(k, carry):
        q_copy(k).start()
        return carry

    lax.fori_loop(1, groups, start_q, 0)
    qr[0] = qs[0]

    loads[1].wait()
    loads[2].wait()
    key_rows = rotated(nn_dot(x, wk[...]))
    leaf_values = nn_dot(x, wv[...]).astype(BF)
    row_id = iota((rows, rows), 0)
    col_id = iota((rows, rows), 1)
    causal = (row_id // leaf_len == col_id // leaf_len) & (col_id <= row_id)
    outs = [[] for _ in range(heads)]
    logs = [[] for _ in range(heads)]
    for h in range(heads):
        span = slice(h * HEAD_DIM, (h + 1) * HEAD_DIM)
        scores = jnp.where(causal, nt_dot(queries[:, span], key_rows[:, span]) * scale, NEG)
        top = jnp.max(scores, axis=1, keepdims=True)
        weights = jnp.exp(scores - top)
        total = jnp.sum(weights, axis=1, keepdims=True)
        outs[h].append(nn_dot(weights.astype(BF), leaf_values[:, span]) / total)
        logs[h].append(top + jnp.log(total))

    loads[4].wait()
    per_chunk = 8
    chunk_rows = per_chunk * slot_rows
    key_id = iota((chunk_rows, keys), 1).astype(F32)
    chunk_lane = iota((chunk_rows, HEAD_DIM), 1)

    def owner_chunk(c, carry):
        def arrived(k, inner):
            q_copy(k).wait_recv()
            return inner

        lax.fori_loop(jnp.maximum(c * per_chunk, 1), (c + 1) * per_chunk, arrived, 0)
        block = qr[pl.ds(c * per_chunk, per_chunk)].reshape(chunk_rows, qs.shape[2])
        meta = block[:, heads * HEAD_DIM :].astype(F32)
        first = meta[:, 0:1] * 32.0 + meta[:, 1:2]
        last = first + meta[:, 2:3] * 32.0 + meta[:, 3:4]
        visible = (key_id >= first) & (key_id < last)
        pieces = []
        tail = jnp.zeros((chunk_rows, HEAD_DIM), F32)
        for h in range(heads):
            span = slice(h * HEAD_DIM, (h + 1) * HEAD_DIM)
            scores = jnp.where(visible, nt_dot(block[:, span], kv[0, :, span]) * scale, NEG)
            top = jnp.max(scores, axis=1, keepdims=True)
            weights = jnp.exp(scores - top)
            total = jnp.sum(weights, axis=1, keepdims=True)
            pieces.append((nn_dot(weights.astype(BF), kv[1, :, span]) / total).astype(BF))
            log_part = top + jnp.log(total)
            log_hi = log_part.astype(BF).astype(F32)
            tail = jnp.where(
                chunk_lane == 2 * h,
                log_hi,
                jnp.where(chunk_lane == 2 * h + 1, log_part - log_hi, tail),
            )
        pieces.append(tail.astype(BF))
        bs[pl.ds(c * per_chunk, per_chunk)] = jnp.concatenate(pieces, axis=1).reshape(
            per_chunk, slot_rows, qs.shape[2]
        )

        def give_back(k, inner):
            b_copy(k).start()
            return inner

        lax.fori_loop(jnp.maximum(c * per_chunk, 1), (c + 1) * per_chunk, give_back, 0)
        return carry

    lax.fori_loop(0, groups // per_chunk, owner_chunk, 0)
    br[0] = bs[0]

    def returned(k, carry):
        b_copy(k).wait_recv()
        return carry

    lax.fori_loop(1, groups, returned, 0)
    back_all = br[...].reshape(groups * slot_rows, qs.shape[2])
    slot_lane = iota((rows, groups * slot_rows), 1).astype(F32)
    for level in range(3):
        pick = (slot_lane == cols[:, level : level + 1]).astype(F32).astype(BF)
        back = nn_dot(pick, back_all)
        for h in range(heads):
            base = heads * HEAD_DIM + 2 * h
            outs[h].append(back[:, h * HEAD_DIM : (h + 1) * HEAD_DIM])
            logs[h].append(back[:, base : base + 1] + back[:, base + 1 : base + 2])
    merged = []
    for h in range(heads):
        top = jnp.maximum(jnp.maximum(logs[h][0], logs[h][1]), jnp.maximum(logs[h][2], logs[h][3]))
        scales = [jnp.exp(one - top) for one in logs[h]]
        weighted = scales[0] * outs[h][0]
        for j in range(1, 4):
            weighted = weighted + scales[j] * outs[h][j]
        merged.append(weighted / (scales[0] + scales[1] + scales[2] + scales[3]))
    attended = jnp.concatenate(merged, axis=1).astype(BF)

    loads[3].wait()
    part[...] = nn_dot(attended, wo[...]).reshape(part.shape)
    total = scatter_sum(p, part, sib_send, sib_recv, rs_send, rs_recv, (r_send, r_recv))
    residual_mid = residual + total
    res_out[...] = residual_mid
    mlp_out[p.t] = rms_rows(residual_mid, gain2[...])
    gather_rows(p, mlp_out, (g2_send, g2_recv))

    def sent(k, carry):
        q_copy(k).wait_send()
        b_copy(k).wait_send()
        return carry

    lax.fori_loop(1, groups, sent, 0)
    for copy in swaps:
        copy.wait()


def moe_kernel(
    mlp, res, table, ein_hbm, eout_hbm, ein_swap, eout_swap, shin_hbm, shout_hbm,
    out,
    win, wout, shin, shout, sb, xb, yb, zb, part, sib_send, sib_recv, rs_send, rs_recv, fs, fr,
    load_sem, d_send, d_recv, y_send, y_recv, r_send, r_recv, f_send, f_recv,
):
    p = Place()
    groups = p.groups
    lanes, shard_rows, width = mlp.shape
    rows = lanes * shard_rows
    cap = sb.shape[1]
    units = shin.shape[1]
    per_chunk = 8
    chunk_rows = per_chunk * cap
    chunks = groups // per_chunk
    requests = out.shape[0]
    leaf_len = rows // requests

    loads = []
    for j, (src, dst) in enumerate(
        (
            (shin_hbm, shin),
            (shout_hbm, shout),
            (ein_hbm.at[p.core], win.at[:, pl.ds(0, units)]),
            (ein_swap, win.at[:, pl.ds(units, units)]),
            (eout_hbm.at[p.core], wout.at[pl.ds(0, units)]),
            (eout_swap, wout.at[pl.ds(units, units)]),
        )
    ):
        copy = pltpu.make_async_copy(src, dst, load_sem.at[j])
        copy.start()
        loads.append(copy)
    announce(p)

    row_id = iota((rows, rows), 0)
    col_id = iota((rows, rows), 1)
    turn = col_id == lax.rem(row_id, requests) * leaf_len + row_id // requests
    x = nn_dot(turn.astype(F32).astype(BF), mlp[...].reshape(rows, width)).astype(BF)

    top_count = 6
    experts = 2 * groups
    expert_id = iota((experts, rows), 0).astype(F32)
    named = [(expert_id == table[k : k + 1, :]).astype(F32) for k in range(top_count)]
    chosen = named[0]
    for k in range(1, top_count):
        chosen = chosen + named[k]
    earlier = (row_id < col_id).astype(F32).astype(BF)
    before = nn_dot(chosen.astype(BF), earlier)
    slot_rows = []
    for k in range(top_count):
        ids = table[k : k + 1, :]
        slot = jnp.sum(named[k] * before, axis=0, keepdims=True)
        group = jnp.floor(ids * 0.5)
        parity = ids - 2.0 * group
        offset = group - p.me.astype(F32)
        offset = jnp.where(offset < 0, offset + groups, offset)
        place = jnp.where(parity == p.core.astype(F32), offset * cap + slot, -1.0)
        slot_rows.append(place)

    def d_copy(k):
        return to_group(sb.at[k], xb.at[k], d_send.at[k], d_recv.at[k], p.ahead(k))

    def y_copy(k):
        return to_group(yb.at[k], zb.at[k], y_send.at[k], y_recv.at[k], p.behind(k))

    chunk_index = iota((chunk_rows, rows), 0).astype(F32)
    await_all(p)

    def pack(c, carry):
        where = chunk_index + (c * chunk_rows).astype(F32)
        pick = (where == slot_rows[0]).astype(F32)
        for k in range(1, top_count):
            pick = pick + (where == slot_rows[k]).astype(F32)
        sb[pl.ds(c * per_chunk, per_chunk)] = (
            nn_dot(pick.astype(BF), x).astype(BF).reshape(per_chunk, cap, width)
        )

        def start(k, inner):
            d_copy(k).start()
            return inner

        lax.fori_loop(jnp.maximum(c * per_chunk, 1), (c + 1) * per_chunk, start, 0)
        return carry

    lax.fori_loop(0, chunks, pack, 0)
    xb[0] = sb[0]

    loads[0].wait()
    loads[1].wait()
    gate = nt_dot(x, shin[0])
    up = nt_dot(x, shin[1])
    hidden = (gate / (1.0 + jnp.exp(-gate)) * up).astype(BF)
    shared = nn_dot(hidden, shout[...])
    own_row = iota((rows, shard_rows), 0)
    own_col = iota((rows, shard_rows), 1)
    mine = (
        lax.rem(own_row, requests) == (shard_rows // leaf_len) * p.t + own_col // leaf_len
    ) & (own_row // requests == lax.rem(own_col, leaf_len))
    shared = shared + jnp.dot(
        mine.astype(F32), res[...], precision=lax.Precision.HIGHEST, preferred_element_type=F32
    )
    part[...] = shared.reshape(part.shape)

    filler = jnp.zeros((rows - 16, rows), F32)
    cols = jnp.transpose(jnp.concatenate([table[...], filler], axis=0), (1, 0))
    slot_cols = jnp.transpose(
        jnp.concatenate(slot_rows + [jnp.zeros((rows - top_count, rows), F32)], axis=0), (1, 0)
    )
    for j in range(2, 6):
        loads[j].wait()

    def compute(c, carry):
        def arrived(k, inner):
            d_copy(k).wait_recv()
            return inner

        lax.fori_loop(jnp.maximum(c * per_chunk, 1), (c + 1) * per_chunk, arrived, 0)
        block = xb[pl.ds(c * per_chunk, per_chunk)].reshape(chunk_rows, width)
        gate_part = nt_dot(block, win[0])
        up_part = nt_dot(block, win[1])
        acted = (gate_part / (1.0 + jnp.exp(-gate_part)) * up_part).astype(BF)
        yb[pl.ds(c * per_chunk, per_chunk)] = (
            nn_dot(acted, wout[...]).astype(BF).reshape(per_chunk, cap, width)
        )

        def start(k, inner):
            y_copy(k).start()
            return inner

        lax.fori_loop(jnp.maximum(c * per_chunk, 1), (c + 1) * per_chunk, start, 0)
        return carry

    lax.fori_loop(0, chunks, compute, 0)
    zb[0] = yb[0]

    slot_lane = iota((rows, chunk_rows), 1).astype(F32)

    def combine(c, carry):
        def arrived(k, inner):
            y_copy(k).wait_recv()
            return inner

        lax.fori_loop(jnp.maximum(c * per_chunk, 1), (c + 1) * per_chunk, arrived, 0)
        where = slot_lane + (c * chunk_rows).astype(F32)
        gates = jnp.zeros((rows, chunk_rows), F32)
        for k in range(top_count):
            gates = gates + jnp.where(
                where == slot_cols[:, k : k + 1], cols[:, 6 + k : 7 + k], 0.0
            )
        high = gates.astype(BF)
        low = (gates - high.astype(F32)).astype(BF)
        block = zb[pl.ds(c * per_chunk, per_chunk)].reshape(chunk_rows, width)
        part[...] += (nn_dot(high, block) + nn_dot(low, block)).reshape(part.shape)
        return carry

    lax.fori_loop(0, chunks, combine, 0)
    total = scatter_sum(p, part, sib_send, sib_recv, rs_send, rs_recv, (r_send, r_recv))
    mixed = total.astype(BF)

    group_row = iota((groups, requests), 0).astype(F32)
    goes = group_row == table[12:13, 0:requests]
    tags = jnp.sum(jnp.where(goes, table[13:14, 0:requests], 0.0), axis=1, keepdims=True)
    outgoing = nn_dot(goes.astype(F32).astype(BF), mixed)
    tagged = jnp.concatenate([outgoing, jnp.broadcast_to(tags, (groups, 128))], axis=1)
    for k in range(groups):
        fs[k] = tagged[k : k + 1]

    def f_copy(k):
        return to_group(fs.at[k], fr.at[k], f_send.at[k], f_recv.at[k], p.ahead(k))

    def f_start(k, carry):
        f_copy(k).start()
        return carry

    lax.fori_loop(1, groups, f_start, 0)
    fr[0] = fs[0]

    def f_wait(k, carry):
        f_copy(k).wait_recv()
        return carry

    lax.fori_loop(1, groups, f_wait, 0)
    landed = jnp.concatenate([fr[k] for k in range(groups)], axis=0)
    place_lane = iota((groups, requests), 1).astype(F32) + 1.0
    settle = (landed[:, width : width + 1] == place_lane).astype(F32).astype(BF)
    out[...] = lax.dot_general(
        settle,
        landed[:, :width].astype(BF),
        (((0,), (0,)), ((), ())),
        preferred_element_type=F32,
    ).astype(BF)

    def sent(k, carry):
        d_copy(k).wait_send()
        y_copy(k).wait_send()
        f_copy(k).wait_send()
        return carry

    lax.fori_loop(1, groups, sent, 0)


def prefix_table(prefix_owner, prefix_start, prefix_len, leaf_len):
    groups = lax.axis_size("dp")
    owner = jnp.transpose(prefix_owner).reshape(-1)
    order = jnp.arange(owner.shape[0])
    twin = (owner[:, None] == owner[None, :]) & (order[None, :] < order[:, None])
    second = jnp.sum(twin.astype(jnp.int32), axis=1)
    offset = lax.rem(owner - lax.axis_index("dp") + groups, groups)
    slot = ((offset * 2 + second) * leaf_len).reshape(3, -1)
    step = jnp.arange(leaf_len, dtype=jnp.int32)

    def spread(values):
        return jnp.repeat(values, leaf_len, axis=1)

    stepping = jnp.tile(step, prefix_owner.shape[0])[None, :]
    lens = jnp.transpose(prefix_len)
    table = jnp.concatenate(
        [
            spread(slot) + stepping,
            spread(jnp.transpose(prefix_start)),
            spread(lens),
            spread(jnp.sum(lens, axis=0, keepdims=True)) + stepping,
        ],
        axis=0,
    )
    return jnp.pad(table, ((0, 6), (0, 0))).astype(F32)


def route_table(expert_ids, gate_weights, request_of):
    groups = lax.axis_size("dp")
    requests, leaf_len, top_count = expert_ids.shape
    rows = requests * leaf_len
    ids = jnp.transpose(expert_ids, (2, 1, 0)).reshape(top_count, rows).astype(F32)
    gates = jnp.transpose(gate_weights, (2, 1, 0)).reshape(top_count, rows)
    offset = lax.rem(request_of // requests - lax.axis_index("dp") + groups, groups)
    place = lax.rem(request_of, requests) + 1
    moves = jnp.pad(jnp.stack([offset, place]), ((0, 2), (0, rows - requests))).astype(F32)
    return jnp.concatenate([ids, gates, moves], axis=0)


def on_device(
    leaf_tokens,
    attn_gain,
    w_query,
    w_key,
    w_value,
    w_out,
    prefix_kv,
    prefix_owner,
    prefix_start,
    prefix_len,
    mlp_gain,
    shared_in,
    shared_out,
    expert_in,
    expert_out,
    expert_ids,
    gate_weights,
    request_of,
):
    groups = lax.axis_size("dp")
    lanes = lax.axis_size("tensor")
    shard_requests, leaf_len, width = leaf_tokens.shape
    requests = prefix_owner.shape[0]
    shard_rows = shard_requests * leaf_len
    local_width = w_query.shape[1]
    units = shared_out.shape[0]
    slot_rows = 2 * leaf_len
    payload = local_width + 128
    cap = 16
    vmem = pl.BlockSpec(memory_space=pltpu.VMEM)
    hbm = pl.BlockSpec(memory_space=pl.ANY)
    dma = pltpu.SemaphoreType.DMA
    ein = jnp.transpose(expert_in, (0, 2, 3, 1))
    table = prefix_table(prefix_owner, prefix_start, prefix_len, leaf_len)
    exchange = pltpu.VMEM((groups, slot_rows, payload), BF)
    block = pltpu.VMEM((4, shard_rows, width), BF)
    part = pltpu.VMEM((lanes, shard_rows, width), F32)
    residual_mid, mlp_rows, ein_swap, eout_swap = pl.pallas_call(
        attention_kernel,
        out_shape=(
            jax.ShapeDtypeStruct((shard_rows, width), F32),
            jax.ShapeDtypeStruct((lanes, shard_rows, width), BF),
            jax.ShapeDtypeStruct(ein.shape[1:], BF),
            jax.ShapeDtypeStruct(expert_out.shape[1:], BF),
        ),
        in_specs=[vmem] * 4 + [hbm] * 7,
        out_specs=(vmem, vmem, hbm, hbm),
        scratch_shapes=[
            pltpu.VMEM(w_query.shape, BF),
            pltpu.VMEM(w_query.shape, BF),
            pltpu.VMEM(w_query.shape, BF),
            pltpu.VMEM(w_out.shape, BF),
            pltpu.VMEM(prefix_kv.shape, BF),
            pltpu.VMEM((lanes, shard_rows, width), BF),
            exchange,
            exchange,
            exchange,
            exchange,
            part,
            block,
            block,
            block,
            block,
            dma((5,)),
            dma((2,)),
            dma((2,)),
            dma((7,)),
            dma((7,)),
            dma((7,)),
            dma((7,)),
            dma((groups,)),
            dma((groups,)),
            dma((groups,)),
            dma((groups,)),
            dma((4,)),
            dma((4,)),
        ],
        compiler_params=pltpu.CompilerParams(
            collective_id=0, has_side_effects=True, vmem_limit_bytes=48 << 20
        ),
        name="attention",
    )(
        leaf_tokens.reshape(shard_rows, width),
        attn_gain.reshape(1, width),
        mlp_gain.reshape(1, width),
        table,
        w_query,
        w_key,
        w_value,
        w_out,
        prefix_kv,
        ein,
        expert_out,
    )
    routes = route_table(expert_ids, gate_weights, request_of)
    rows_in = pltpu.VMEM((groups, cap, width), BF)
    final = pltpu.VMEM((groups, 1, width + 128), F32)
    mixed = pl.pallas_call(
        moe_kernel,
        out_shape=jax.ShapeDtypeStruct((requests, width), BF),
        in_specs=[vmem] * 3 + [hbm] * 6,
        out_specs=vmem,
        scratch_shapes=[
            pltpu.VMEM((2, 2 * units, width), BF),
            pltpu.VMEM((2 * units, width), BF),
            pltpu.VMEM((2, units, width), BF),
            pltpu.VMEM((units, width), BF),
            rows_in,
            rows_in,
            rows_in,
            rows_in,
            part,
            block,
            block,
            block,
            block,
            final,
            final,
            dma((6,)),
            dma((groups,)),
            dma((groups,)),
            dma((groups,)),
            dma((groups,)),
            dma((4,)),
            dma((4,)),
            dma((groups,)),
            dma((groups,)),
        ],
        compiler_params=pltpu.CompilerParams(
            collective_id=1, has_side_effects=True, vmem_limit_bytes=48 << 20
        ),
        name="experts",
    )(
        mlp_rows,
        residual_mid,
        routes,
        ein,
        expert_out,
        ein_swap,
        eout_swap,
        jnp.transpose(shared_in, (1, 2, 0)),
        shared_out,
    )
    return mixed.reshape(requests, 1, width)


def solution(mesh):
    in_specs = (
        P(("dp", "tensor"), None, None),
        P(),
        P(None, "tensor"),
        P(None, "tensor"),
        P(None, "tensor"),
        P("tensor", None),
        P(None, "dp", "tensor"),
        P("dp", None),
        P("dp", None),
        P("dp", None),
        P(),
        P(None, None, "tensor"),
        P("tensor", None),
        P("dp", None, None, "tensor"),
        P("dp", "tensor", None),
        P("dp", None, None),
        P("dp", None, None),
        P("dp"),
    )
    out_specs = P("dp", "tensor", None)
    return jax.shard_map(
        on_device, mesh=mesh, in_specs=in_specs, out_specs=out_specs, check_vma=False
    )
```

time: 652 us -> 212 us (0.33)
  the two profiles are of different devices: /device:TPU:2 before, /device:TPU:32 now
where the time goes in v1:
time: 212 us; the launch traced here: 211 us
  Pallas kernels  195 us (92%)
  local copies, waits for them, and re-layouts  12.8 us (6%)
  other arithmetic  3.11 us (1%)
    pallas_call x1, Pallas kernels, on_device(): pl.pallas_call(moe_kernel, out_shape=jax.ShapeDtypeStruct((requests, widt...  131 us
    pallas_call x1, Pallas kernels, on_device(): pl.pallas_call(attention_kernel, out_shape=(jax.ShapeDtypeStruct((shard_r...  63.7 us
    unnamed x21, local copies, waits for them, and re-layouts  9.07 us

profile of v1, /device:TPU:32, one launch (start us, length us, event | category | flops | bytes accessed | tf_op | source)
XLA Modules:
  0.0 210.9 jit_solution(1627911796469560635)
XLA Ops:
  0.0 0.8 eq.15
  0.8 0.2 convert_reduce_fusion
  0.9 0.7 reduce_sum.22
  1.6 0.7 fusion.6
  2.3 0.1 reduce_sum.21
  2.4 0.7 fusion.4
  3.1 0.8 reshape.63
  3.9 0.1 iota_add_fusion
  4.0 0.1 add.49
  4.1 0.1 add.45
  4.2 0.1 broadcast_in_dim.15
  4.3 0.1 reshape.60
  4.4 0.8 broadcast_in_dim.16
  5.1 0.1 reshape.61
  5.2 0.7 convert_bitcast_fusion
  6.0 0.1 convert_element_type.22
  6.1 0.8 broadcast_in_dim.17
  6.8 0.1 reshape.62
  6.9 0.0 copy-start.2
  6.9 1.2 copy-done.2
  8.2 0.0 copy-start.3
  8.2 1.2 copy-done.3
  9.4 0.0 copy-start.4
  9.4 1.2 copy-done.4
  10.6 0.0 copy-start.5
  10.6 1.2 copy-done.5
  11.8 0.0 copy-start.7
  11.8 0.8 copy-done.7
  12.6 0.0 copy-start.8
  12.6 0.7 copy-done.8
  13.3 0.0 copy-start.9
  13.3 0.7 copy-done.9
  14.0 0.0 copy-start
  14.0 0.0 copy-start.6
  14.0 63.7 %attention.1 = (f32[16,2048]{1,0:T(8,128)S(1)}, bf16[8,16,2048]{2,1,0:T(8,128)(2,1)S(1)}, bf16[2,176,2048]{2,1,0:T(8,128)(2,1)}, bf16[176,2048]{1,0:T(8,128)(2,1)S(1)}) custom-call(bf16[16,2048]{1,0:T(8,128)(2,1)S(1)} %bitcast.18, f32[1,2048]{1,0:T(1,128)S(1)} %bitcast.19, f32[1,2048]{1,0:T(1,128)S(1)} %bitcast.20, f32[16,128]{1,0:T(8,128)S(1)} %pad_convert_fusion.table, ...), custom_call_target="tpu_custom_call" | custom-call | tf_op jit(solution)/shard_map/attention/pallas_call | solution.py:608
  77.8 0.0 copy-done
  77.8 0.0 copy-done.6
  77.8 0.0 copy-start.1
  77.8 1.4 copy-done.1
  79.2 131.1 %experts.1 = bf16[16,2048]{1,0:T(8,128)(2,1)S(1)} custom-call(bf16[8,16,2048]{2,1,0:T(8,128)(2,1)S(1)} %get-tuple-element.9.mlp, f32[16,2048]{1,0:T(8,128)S(1)} %get-tuple-element.10.res, f32[16,128]{1,0:T(8,128)S(1)} %pad_maximum_fusion.table, bf16[2,2,176,2048]{3,2,1,0:T(8,128)(2,1)} %bitcast.22, bf16[2,176,2048]{2,1,0:T(8,128)(2,1)S(1)} %copy-done, ...), custom_call_target="tpu_custom_call" | custom-call | tf_op jit(solution)/shard_map/experts/pallas_call | solution.py:668
  210.3 0.6 copy.20
  (7 shorter events, 0.1 us)
Async XLA Ops:
  6.9 1.2 copy-start.2
  8.2 1.2 copy-start.3
  9.4 1.2 copy-start.4
  10.6 1.2 copy-start.5
  11.8 0.8 copy-start.7
  12.6 0.7 copy-start.8
  13.3 0.7 copy-start.9
  14.0 63.7 %copy-start = (bf16[2,176,2048]{2,1,0:T(8,128)(2,1)S(1)}, bf16[2,176,2048]{2,1,0:T(8,128)(2,1)}, u32[]{:S(2)}) copy-start(bf16[2,176,2048]{2,1,0:T(8,128)(2,1)} %eout_hbm.3) | copy-start | bytes 4325380
  14.0 63.8 %copy-start.6 = (bf16[176,2048]{1,0:T(8,128)(2,1)S(1)}, bf16[176,2048]{1,0:T(8,128)(2,1)}, u32[]{:S(2)}) copy-start(bf16[176,2048]{1,0:T(8,128)(2,1)} %shout_hbm.1) | copy-start | bytes 2162692
  77.8 1.4 copy-start.1

commit v2 on v1

v2 whole, which is shorter than its diff:
```python
import jax
import jax.numpy as jnp
from jax import lax
from jax.experimental import pallas as pl
from jax.experimental.pallas import tpu as pltpu
from jax.sharding import PartitionSpec as P

HEAD_DIM = 128
EPS = 1e-06
ROPE_BASE = 10000.0
CAP = 16
MESH = pl.DeviceIdType.MESH
BF = jnp.bfloat16
F32 = jnp.float32
NEG = -1e30


def nt_dot(a, b):
    return lax.dot_general(a, b, (((1,), (1,)), ((), ())), preferred_element_type=F32)


def nn_dot(a, b):
    return jnp.dot(a, b, preferred_element_type=F32)


def exact_dot(a, b):
    return jnp.dot(a, b, precision=lax.Precision.HIGHEST, preferred_element_type=F32)


def onehot(mask):
    return mask.astype(F32).astype(BF)


def rms_rows(values, gain):
    mean_square = jnp.mean(values * values, axis=-1, keepdims=True)
    return (values * lax.rsqrt(mean_square + EPS) * gain).astype(BF)


def iota(shape, dim):
    return lax.broadcasted_iota(jnp.int32, shape, dim)


class Place:
    def __init__(self):
        self.groups = lax.axis_size("dp")
        self.me = lax.axis_index("dp")
        self.t = lax.axis_index("tensor")
        self.chip = self.t // 2
        self.core = lax.rem(self.t, 2)
        self.sib = self.chip * 2 + (1 - self.core)
        self.half = lax.rem(self.me, 2)
        self.spot = self.me // 2
        self.spots = self.groups // 2
        self.mirror = self.spot * 2 + (1 - self.half)

    def ahead(self, k):
        return lax.rem(self.me + k, self.groups)

    def behind(self, k):
        return lax.rem(self.me + self.groups - k, self.groups)

    def spot_ahead(self, k):
        return lax.rem(self.spot + k, self.spots) * 2 + self.half

    def spot_behind(self, k):
        return lax.rem(self.spot + self.spots - k, self.spots) * 2 + self.half

    def lane(self, k):
        return lax.rem(self.chip + k, 4) * 2 + self.core


def to_group(src, dst, send, recv, group):
    return pltpu.make_async_remote_copy(
        src, dst, send, recv, device_id={"dp": group}, device_id_type=MESH
    )


def to_lane(src, dst, send, recv, lane):
    return pltpu.make_async_remote_copy(
        src, dst, send, recv, device_id={"tensor": lane}, device_id_type=MESH
    )


def to_both(src, dst, send, recv, group, lane):
    return pltpu.make_async_remote_copy(
        src, dst, send, recv, device_id={"dp": group, "tensor": lane}, device_id_type=MESH
    )


def announce(p):
    barrier = pltpu.get_barrier_semaphore()

    def signal(k, carry):
        pl.semaphore_signal(barrier, inc=1, device_id={"dp": p.ahead(k)}, device_id_type=MESH)
        return carry

    pl.semaphore_signal(barrier, inc=1, device_id={"tensor": p.sib}, device_id_type=MESH)
    for k in range(1, 4):
        pl.semaphore_signal(barrier, inc=1, device_id={"tensor": p.lane(k)}, device_id_type=MESH)
        pl.semaphore_signal(
            barrier,
            inc=1,
            device_id={"dp": p.mirror, "tensor": p.lane(k)},
            device_id_type=MESH,
        )
    lax.fori_loop(1, p.groups, signal, 0)


def await_all(p):
    pl.semaphore_wait(pltpu.get_barrier_semaphore(), p.groups - 1 + 7)


def gather_rows(p, buf, sems, between=None):
    send, recv = sems
    direct = []
    for k in range(1, 4):
        copy = to_lane(buf.at[p.t], buf.at[p.t], send.at[k], recv.at[k], p.lane(k))
        copy.start()
        direct.append(copy)
    passed = [to_lane(buf.at[p.t], buf.at[p.t], send.at[0], recv.at[0], p.sib)]
    passed[0].start()
    if between is not None:
        between()
    for k in range(1, 4):
        direct[k - 1].wait_recv()
        source = p.lane(4 - k)
        copy = to_lane(buf.at[source], buf.at[source], send.at[3 + k], recv.at[3 + k], p.sib)
        copy.start()
        passed.append(copy)
    for copy in direct:
        copy.wait_send()
    for copy in passed:
        copy.wait()


def gather_column(p, buf, sems, between=None):
    send, recv = sems
    direct = []
    for k in range(1, 4):
        direct.append(
            to_lane(buf.at[0, p.t], buf.at[0, p.t], send.at[k], recv.at[k], p.lane(k))
        )
        direct[-1].start()
    for k in range(4):
        direct.append(
            to_both(
                buf.at[0, p.t], buf.at[1, p.t], send.at[4 + k], recv.at[4 + k], p.mirror, p.lane(k)
            )
        )
        direct[-1].start()
    passed = [to_lane(buf.at[0, p.t], buf.at[0, p.t], send.at[0], recv.at[0], p.sib)]
    passed[0].start()
    if between is not None:
        between()
    for j in range(7):
        origin, k = (0, j + 1) if j < 3 else (1, j - 3)
        direct[j].wait_recv()
        block = buf.at[origin, p.lane(4 - k)]
        copy = to_lane(block, block, send.at[8 + j], recv.at[8 + j], p.sib)
        copy.start()
        passed.append(copy)
    for copy in direct:
        copy.wait_send()
    for copy in passed:
        copy.wait()


def scatter_sum(p, part, sib_send, sib_recv, rs_send, rs_recv, sems):
    send, recv = sems
    for c in range(4):
        sib_send[c] = part[:, c * 2 + (1 - p.core)].astype(BF)
    swap = to_lane(sib_send, sib_recv, send.at[0], recv.at[0], p.sib)
    swap.start()
    swap.wait_recv()
    copies = []
    for k in range(1, 4):
        there = lax.rem(p.chip + k, 4)
        rs_send[k - 1] = (part[:, there * 2 + p.core] + sib_recv[there].astype(F32)).astype(BF)
        copy = to_lane(rs_send.at[k - 1], rs_recv.at[k - 1], send.at[k], recv.at[k], p.lane(k))
        copy.start()
        copies.append(copy)
    total = part[:, p.t] + sib_recv[p.chip].astype(F32)
    for k in range(1, 4):
        copies[k - 1].wait_recv()
        total = total + rs_recv[k - 1].astype(F32)
    swap.wait_send()
    for copy in copies:
        copy.wait_send()
    return total


def each(first, last, action):
    def step(k, carry):
        action(k)
        return carry

    lax.fori_loop(first, last, step, 0)


def layer_kernel(
    leaf_hbm, gain1_hbm, gain2_hbm, owner_hbm, start_hbm, count_hbm, wq_hbm, wk_hbm, wv_hbm,
    wo_hbm, kv_hbm, ids_hbm, gates_hbm, moves_hbm, shin_hbm, shout_hbm, ein_hbm, eout_hbm,
    out,
    leaf, gain1, gain2, owner, start, count, wq, wk, wv, wo, kv, ids, gates, moves, shin, shout,
    win, wout, xg, qs, qr, bs, br, part1, sib_send1, sib_recv1, rs_send1, rs_recv1,
    rows2, sb, xb, yb, zb, part2, sib_send2, sib_recv2, rs_send2, rs_recv2,
    cross_send, cross_recv, fs, fr,
    load_sem, swap_send, swap_recv, g1_send, g1_recv, g2_send, g2_recv,
    q_send, q_recv, b_send, b_recv, r1_send, r1_recv,
    d_send, d_recv, y_send, y_recv, r2_send, r2_recv, f_send, f_recv,
):
    p = Place()
    groups = p.groups
    lanes, shard_rows, width = xg.shape
    rows = lanes * shard_rows
    heads = wq.shape[1] // HEAD_DIM
    slot_rows = qs.shape[1]
    leaf_len = slot_rows // 2
    keys = kv.shape[1]
    units = shin.shape[1]
    requests = out.shape[0]
    top_count = ids.shape[1]
    scale = HEAD_DIM**-0.5
    other = 1 - p.core

    loads = {}
    for j, (name, src, dst) in enumerate(
        (
            ("leaf", leaf_hbm, leaf),
            ("gain1", gain1_hbm, gain1),
            ("owner", owner_hbm, owner),
            ("start", start_hbm, start),
            ("count", count_hbm, count),
            ("wq", wq_hbm, wq),
            ("wk", wk_hbm, wk),
            ("wv", wv_hbm, wv),
            ("kv", kv_hbm, kv),
            ("wo", wo_hbm, wo),
            ("gain2", gain2_hbm, gain2),
            ("ids", ids_hbm, ids.at[0]),
            ("gates", gates_hbm, gates.at[0]),
            ("moves", moves_hbm, moves),
            ("shin", shin_hbm, shin),
            ("shout", shout_hbm, shout),
            ("ein", ein_hbm.at[p.core], win.at[:, pl.ds(0, units)]),
            ("eout", eout_hbm.at[p.core], wout.at[pl.ds(0, units)]),
        )
    ):
        loads[name] = pltpu.make_async_copy(src, dst, load_sem.at[j])
        loads[name].start()
    announce(p)
    loads["leaf"].wait()
    loads["gain1"].wait()
    residual = leaf[...].astype(F32)
    xg[p.t] = rms_rows(residual, gain1[...])
    await_all(p)
    swaps = [
        to_lane(
            ein_hbm.at[other], win.at[:, pl.ds(units, units)], swap_send.at[0], swap_recv.at[0], p.sib
        ),
        to_lane(
            eout_hbm.at[other], wout.at[pl.ds(units, units)], swap_send.at[1], swap_recv.at[1], p.sib
        ),
        to_group(ids_hbm, ids.at[1], swap_send.at[2], swap_recv.at[2], p.mirror),
        to_group(gates_hbm, gates.at[1], swap_send.at[3], swap_recv.at[3], p.mirror),
    ]

    lane = iota((rows, HEAD_DIM), 1)
    lane_row = iota((1, rows), 1)
    row_id = iota((rows, rows), 0)
    col_id = iota((rows, rows), 1)
    half = HEAD_DIM // 2
    made = {}

    def tables():
        for name in ("owner", "start", "count"):
            loads[name].wait()
        spread = (iota((requests, rows), 1) // leaf_len == iota((requests, rows), 0)).astype(F32)
        owners = exact_dot(owner[...].astype(F32), spread)
        starts = exact_dot(start[...].astype(F32), spread)
        counts = exact_dot(count[...].astype(F32), spread)
        step = lax.rem(lane_row, leaf_len).astype(F32)
        position = jnp.sum(counts, axis=0, keepdims=True) + step
        first_cols = jnp.transpose(
            jnp.concatenate(
                [owners, starts, counts, position, jnp.zeros((6, rows), F32)], axis=0
            ),
            (1, 0),
        )
        slots = []
        for level in range(3):
            mine = owners[level : level + 1, :]
            second = jnp.zeros((1, rows), F32)
            for above in range(level):
                same = (first_cols[:, above : above + 1] == mine).astype(F32)
                second = jnp.maximum(second, jnp.max(same, axis=0, keepdims=True))
            offset = mine - p.me.astype(F32)
            offset = jnp.where(offset < 0, offset + groups, offset)
            slots.append((offset * 2.0 + second) * leaf_len + step)
        made["slots"] = slots
        made["slot_cols"] = jnp.transpose(
            jnp.concatenate(slots + [jnp.zeros((5, rows), F32)], axis=0), (1, 0)
        )
        frequency = jnp.exp(
            (-2.0 / HEAD_DIM * jnp.log(ROPE_BASE)) * lax.rem(lane, half).astype(F32)
        )
        angles = first_cols[:, 9:10] * frequency
        made["cosine"] = jnp.cos(angles)
        made["sine"] = jnp.where(lane < half, -1.0, 1.0) * jnp.sin(angles)
        made["cols"] = first_cols
        slot_index = iota((groups * slot_rows, rows), 0).astype(F32)
        made["places"] = jnp.concatenate([onehot(slot_index == one) for one in slots], axis=1)
        metas = []
        for level in range(3):
            begin = first_cols[:, 3 + level : 4 + level]
            length = first_cols[:, 6 + level : 7 + level]
            begin_hi = jnp.floor(begin * (1.0 / 32.0))
            length_hi = jnp.floor(length * (1.0 / 32.0))
            meta = jnp.where(lane == 3, length - 32.0 * length_hi, 0.0)
            meta = jnp.where(lane == 2, length_hi, meta)
            meta = jnp.where(lane == 1, begin - 32.0 * begin_hi, meta)
            metas.append(jnp.where(lane == 0, begin_hi, meta).astype(BF))
        made["metas"] = metas

    gather_rows(p, xg, (g1_send, g1_recv), tables)
    for copy in swaps:
        copy.start()
    cosine, sine = made["cosine"], made["sine"]

    def rotated(values):
        pieces = []
        for h in range(heads):
            one = values[:, h * HEAD_DIM : (h + 1) * HEAD_DIM]
            pieces.append(one * cosine + pltpu.roll(one, half, 1) * sine)
        return jnp.concatenate(pieces, axis=1).astype(BF)

    x = xg[...].reshape(rows, width)
    loads["wq"].wait()
    queries = rotated(nn_dot(x, wq[...]))
    stacked = jnp.concatenate(
        [jnp.concatenate([queries, meta], axis=1) for meta in made["metas"]], axis=0
    )
    qs[...] = nn_dot(made["places"], stacked).astype(BF).reshape(qs.shape)

    def q_copy(k):
        return to_group(qs.at[k], qr.at[k], q_send.at[k], q_recv.at[k], p.ahead(k))

    def b_copy(k):
        return to_group(bs.at[k], br.at[k], b_send.at[k], b_recv.at[k], p.behind(k))

    each(1, groups, lambda k: q_copy(k).start())
    qr[0] = qs[0]

    loads["wk"].wait()
    loads["wv"].wait()
    key_rows = rotated(nn_dot(x, wk[...]))
    leaf_values = nn_dot(x, wv[...]).astype(BF)
    causal = (row_id // leaf_len == col_id // leaf_len) & (col_id <= row_id)
    outs = [[] for _ in range(heads)]
    logs = [[] for _ in range(heads)]
    for h in range(heads):
        span = slice(h * HEAD_DIM, (h + 1) * HEAD_DIM)
        scores = jnp.where(causal, nt_dot(queries[:, span], key_rows[:, span]) * scale, NEG)
        top = jnp.max(scores, axis=1, keepdims=True)
        weights = jnp.exp(scores - top)
        total = jnp.sum(weights, axis=1, keepdims=True)
        outs[h].append(nn_dot(weights.astype(BF), leaf_values[:, span]) / total)
        logs[h].append(top + jnp.log(total))

    loads["kv"].wait()
    per_chunk = 8
    chunk_rows = per_chunk * slot_rows
    key_id = iota((chunk_rows, keys), 1).astype(F32)
    chunk_lane = iota((chunk_rows, HEAD_DIM), 1)

    def owner_chunk(c):
        first_k, last_k = jnp.maximum(c * per_chunk, 1), (c + 1) * per_chunk
        each(first_k, last_k, lambda k: q_copy(k).wait_recv())
        block = qr[pl.ds(c * per_chunk, per_chunk)].reshape(chunk_rows, qs.shape[2])
        meta = block[:, heads * HEAD_DIM :].astype(F32)
        first = meta[:, 0:1] * 32.0 + meta[:, 1:2]
        last = first + meta[:, 2:3] * 32.0 + meta[:, 3:4]
        visible = (key_id >= first) & (key_id < last)
        pieces = []
        tail = jnp.zeros((chunk_rows, HEAD_DIM), F32)
        for h in range(heads):
            span = slice(h * HEAD_DIM, (h + 1) * HEAD_DIM)
            scores = jnp.where(visible, nt_dot(block[:, span], kv[0, :, span]) * scale, NEG)
            top = jnp.max(scores, axis=1, keepdims=True)
            weights = jnp.exp(scores - top)
            total = jnp.sum(weights, axis=1, keepdims=True)
            pieces.append((nn_dot(weights.astype(BF), kv[1, :, span]) / total).astype(BF))
            log_part = top + jnp.log(total)
            log_hi = log_part.astype(BF).astype(F32)
            tail = jnp.where(chunk_lane == 2 * h, log_hi, tail)
            tail = jnp.where(chunk_lane == 2 * h + 1, log_part - log_hi, tail)
        pieces.append(tail.astype(BF))
        bs[pl.ds(c * per_chunk, per_chunk)] = jnp.concatenate(pieces, axis=1).reshape(
            per_chunk, slot_rows, qs.shape[2]
        )
        each(first_k, last_k, lambda k: b_copy(k).start())

    each(0, groups // per_chunk, owner_chunk)
    br[0] = bs[0]
    slot_lane = iota((rows, groups * slot_rows), 1).astype(F32)
    picks = [
        onehot(slot_lane == made["slot_cols"][:, level : level + 1]) for level in range(3)
    ]
    each(1, groups, lambda k: b_copy(k).wait_recv())
    back_all = br[...].reshape(groups * slot_rows, qs.shape[2])
    for level in range(3):
        back = nn_dot(picks[level], back_all)
        for h in range(heads):
            base = heads * HEAD_DIM + 2 * h
            outs[h].append(back[:, h * HEAD_DIM : (h + 1) * HEAD_DIM])
            logs[h].append(back[:, base : base + 1] + back[:, base + 1 : base + 2])
    merged = []
    for h in range(heads):
        top = jnp.maximum(jnp.maximum(logs[h][0], logs[h][1]), jnp.maximum(logs[h][2], logs[h][3]))
        scales = [jnp.exp(one - top) for one in logs[h]]
        weighted = scales[0] * outs[h][0]
        for j in range(1, 4):
            weighted = weighted + scales[j] * outs[h][j]
        merged.append(weighted / (scales[0] + scales[1] + scales[2] + scales[3]))
    attended = jnp.concatenate(merged, axis=1).astype(BF)

    loads["wo"].wait()
    part1[...] = nn_dot(attended, wo[...]).reshape(part1.shape)
    total = scatter_sum(p, part1, sib_send1, sib_recv1, rs_send1, rs_recv1, (r1_send, r1_recv))
    residual_mid = residual + total[0]
    loads["gain2"].wait()
    rows2[0, p.t] = rms_rows(residual_mid, gain2[...])

    tokens = 2 * rows
    wide_row = iota((tokens, tokens), 0)
    wide_col = iota((tokens, tokens), 1)
    routes = {}

    def routing():
        loads["ids"].wait()
        loads["gates"].wait()
        swaps[2].wait()
        swaps[3].wait()
        tile = onehot(lax.rem(iota((requests, rows), 1), requests) == iota((requests, rows), 0))
        spots = top_count * leaf_len
        own = (
            lax.rem(iota((spots, rows), 0), leaf_len) == iota((spots, rows), 1) // requests
        ).astype(F32)

        def line(values):
            wide = nn_dot(values.astype(BF), tile) * own
            return jnp.sum(wide.reshape(top_count, leaf_len, rows), axis=1)

        id_lines, gate_lines = [], []
        for origin in range(2):
            id_lines.append(line(ids[origin].reshape(spots, requests).astype(F32)))
            gate = gates[origin].reshape(spots, requests)
            gate_hi = gate.astype(BF).astype(F32)
            gate_lines.append(line(gate_hi) + line(gate - gate_hi))
        id_line = jnp.concatenate(id_lines, axis=1)
        gate_line = jnp.concatenate(gate_lines, axis=1)
        expert_id = iota((2 * groups, tokens), 0).astype(F32)
        named = [(expert_id == id_line[k : k + 1, :]).astype(F32) for k in range(top_count)]
        chosen = named[0]
        for k in range(1, top_count):
            chosen = chosen + named[k]
        earlier = onehot((wide_row < wide_col) & (wide_row // rows == wide_col // rows))
        before = nn_dot(chosen.astype(BF), earlier)
        origin_row = (iota((1, tokens), 1) // rows).astype(F32)
        slots = []
        for k in range(top_count):
            one = id_line[k : k + 1, :]
            slot = jnp.sum(named[k] * before, axis=0, keepdims=True)
            group = jnp.floor(one * 0.5)
            spot = jnp.floor(one * 0.25)
            here = (one - 2.0 * group == p.core.astype(F32)) & (
                group - 2.0 * spot == p.half.astype(F32)
            )
            offset = spot - p.spot.astype(F32)
            offset = jnp.where(offset < 0, offset + p.spots, offset)
            slots.append(jnp.where(here, (offset * 2.0 + origin_row) * CAP + slot, -1.0))
        routes["slots"] = slots
        routes["cols"] = jnp.transpose(
            jnp.concatenate(slots + [gate_line, jnp.zeros((4, tokens), F32)], axis=0), (1, 0)
        )

    gather_column(p, rows2, (g2_send, g2_recv), routing)
    turn = onehot(
        wide_col
        == wide_row // rows * rows
        + lax.rem(wide_row, requests) * leaf_len
        + lax.rem(wide_row, rows) // requests
    )
    x = nn_dot(turn, rows2[...].reshape(tokens, width)).astype(BF)

    cap = sb.shape[1]
    per_chunk2 = 4
    chunk2 = per_chunk2 * cap

    def d_copy(k):
        return to_group(sb.at[k], xb.at[k], d_send.at[k], d_recv.at[k], p.spot_ahead(k))

    def y_copy(k):
        return to_group(yb.at[k], zb.at[k], y_send.at[k], y_recv.at[k], p.spot_behind(k))

    chunk_index = iota((chunk2, tokens), 0).astype(F32)

    def pack(c):
        where = chunk_index + (c * chunk2).astype(F32)
        pick = (where == routes["slots"][0]).astype(F32)
        for k in range(1, top_count):
            pick = pick + (where == routes["slots"][k]).astype(F32)
        sb[pl.ds(c * per_chunk2, per_chunk2)] = (
            nn_dot(pick.astype(BF), x).astype(BF).reshape(per_chunk2, cap, width)
        )
        each(
            jnp.maximum(c * per_chunk2, 1), (c + 1) * per_chunk2, lambda k: d_copy(k).start()
        )

    each(0, p.spots // per_chunk2, pack)
    xb[0] = sb[0]

    loads["shin"].wait()
    loads["shout"].wait()
    x_own = x[:rows]
    gate = nt_dot(x_own, shin[0])
    up = nt_dot(x_own, shin[1])
    hidden = (gate / (1.0 + jnp.exp(-gate)) * up).astype(BF)
    shared = nn_dot(hidden, shout[...])
    own_row = iota((rows, shard_rows), 0)
    own_col = iota((rows, shard_rows), 1)
    mine = (
        lax.rem(own_row, requests) == (shard_rows // leaf_len) * p.t + own_col // leaf_len
    ) & (own_row // requests == lax.rem(own_col, leaf_len))
    shared = shared + exact_dot(mine.astype(F32), residual_mid)
    part2[0] = shared.reshape(part2.shape[1:])
    part2[1] = jnp.zeros(part2.shape[1:], F32)

    loads["ein"].wait()
    loads["eout"].wait()
    swaps[0].wait()
    swaps[1].wait()

    def compute(c):
        first_k, last_k = jnp.maximum(c * per_chunk2, 1), (c + 1) * per_chunk2
        each(first_k, last_k, lambda k: d_copy(k).wait_recv())
        block = xb[pl.ds(c * per_chunk2, per_chunk2)].reshape(chunk2, width)
        gate_part = nt_dot(block, win[0])
        up_part = nt_dot(block, win[1])
        acted = (gate_part / (1.0 + jnp.exp(-gate_part)) * up_part).astype(BF)
        yb[pl.ds(c * per_chunk2, per_chunk2)] = (
            nn_dot(acted, wout[...]).astype(BF).reshape(per_chunk2, cap, width)
        )
        each(first_k, last_k, lambda k: y_copy(k).start())

    each(0, p.spots // per_chunk2, compute)
    zb[0] = yb[0]
    token_lane = iota((tokens, chunk2), 1).astype(F32)

    def combine(c):
        first_k, last_k = jnp.maximum(c * per_chunk2, 1), (c + 1) * per_chunk2
        each(first_k, last_k, lambda k: y_copy(k).wait_recv())
        where = token_lane + (c * chunk2).astype(F32)
        weights = jnp.zeros((tokens, chunk2), F32)
        for k in range(top_count):
            weights = weights + jnp.where(
                where == routes["cols"][:, k : k + 1],
                routes["cols"][:, top_count + k : top_count + k + 1],
                0.0,
            )
        high = weights.astype(BF)
        low = (weights - high.astype(F32)).astype(BF)
        block = zb[pl.ds(c * per_chunk2, per_chunk2)].reshape(chunk2, width)
        part2[...] += (nn_dot(high, block) + nn_dot(low, block)).reshape(part2.shape)

    each(0, p.spots // per_chunk2, combine)
    total = scatter_sum(p, part2, sib_send2, sib_recv2, rs_send2, rs_recv2, (r2_send, r2_recv))
    cross_send[...] = total[1].astype(BF)
    cross = to_group(cross_send, cross_recv, f_send.at[0], f_recv.at[0], p.mirror)
    cross.start()

    loads["moves"].wait()
    target = moves[...]
    aim = lax.rem(target // requests - p.me + groups, groups)
    spot_tag = lax.rem(target, requests) + 1
    goes = iota((groups, requests), 0) == aim
    tags = jnp.sum(jnp.where(goes, spot_tag.astype(F32), 0.0), axis=1, keepdims=True)
    cross.wait_recv()
    mixed = (total[0] + cross_recv[...].astype(F32)).astype(BF)
    outgoing = nn_dot(onehot(goes), mixed)
    tagged = jnp.concatenate([outgoing, jnp.broadcast_to(tags, (groups, 128))], axis=1)
    for k in range(groups):
        fs[k] = tagged[k : k + 1]

    def f_copy(k):
        return to_group(fs.at[k], fr.at[k], f_send.at[k], f_recv.at[k], p.ahead(k))

    each(1, groups, lambda k: f_copy(k).start())
    fr[0] = fs[0]
    each(1, groups, lambda k: f_copy(k).wait_recv())
    landed = jnp.concatenate([fr[k] for k in range(groups)], axis=0)
    place_lane = iota((groups, requests), 1).astype(F32) + 1.0
    settle = onehot(landed[:, width : width + 1] == place_lane)
    out[...] = lax.dot_general(
        settle,
        landed[:, :width].astype(BF),
        (((0,), (0,)), ((), ())),
        preferred_element_type=F32,
    ).astype(BF)

    cross.wait_send()

    def sent(k):
        q_copy(k).wait_send()
        b_copy(k).wait_send()
        f_copy(k).wait_send()

    def sent2(k):
        d_copy(k).wait_send()
        y_copy(k).wait_send()

    each(1, groups, sent)
    each(1, p.spots, sent2)


def on_device(
    leaf_tokens,
    attn_gain,
    w_query,
    w_key,
    w_value,
    w_out,
    prefix_kv,
    prefix_owner,
    prefix_start,
    prefix_len,
    mlp_gain,
    shared_in,
    shared_out,
    expert_in,
    expert_out,
    expert_ids,
    gate_weights,
    request_of,
):
    groups = lax.axis_size("dp")
    lanes = lax.axis_size("tensor")
    shard_requests, leaf_len, width = leaf_tokens.shape
    requests = prefix_owner.shape[0]
    shard_rows = shard_requests * leaf_len
    local_width = w_query.shape[1]
    units = shared_out.shape[0]
    top_count = expert_ids.shape[2]
    slot_rows = 2 * leaf_len
    payload = local_width + 128
    hbm = pl.BlockSpec(memory_space=pltpu.HBM)
    dma = pltpu.SemaphoreType.DMA
    vm = pltpu.VMEM
    exchange = vm((groups, slot_rows, payload), BF)
    table = vm((3, requests), jnp.int32)
    weight = vm(w_query.shape, BF)
    block1 = vm((4, 1, shard_rows, width), BF)
    block2 = vm((4, 2, shard_rows, width), BF)
    rows_in = vm((groups // 2, 2 * CAP, width), BF)
    final = vm((groups, 1, width + 128), F32)
    column = (2, top_count, leaf_len, requests)
    mixed = pl.pallas_call(
        layer_kernel,
        out_shape=jax.ShapeDtypeStruct((requests, width), BF),
        in_specs=[hbm] * 18,
        out_specs=pl.BlockSpec(memory_space=pltpu.VMEM),
        scratch_shapes=[
            vm((shard_rows, width), BF),
            vm((1, width), F32),
            vm((1, width), F32),
            table,
            table,
            table,
            weight,
            weight,
            weight,
            vm(w_out.shape, BF),
            vm(prefix_kv.shape, BF),
            vm(column, jnp.int32),
            vm(column, F32),
            vm((1, requests), jnp.int32),
            vm((2, units, width), BF),
            vm((units, width), BF),
            vm((2, 2 * units, width), BF),
            vm((2 * units, width), BF),
            vm((lanes, shard_rows, width), BF),
            exchange,
            exchange,
            exchange,
            exchange,
            vm((1, lanes, shard_rows, width), F32),
            block1,
            block1,
            block1,
            block1,
            vm((2, lanes, shard_rows, width), BF),
            rows_in,
            rows_in,
            rows_in,
            rows_in,
            vm((2, lanes, shard_rows, width), F32),
            block2,
            block2,
            block2,
            block2,
            vm((shard_rows, width), BF),
            vm((shard_rows, width), BF),
            final,
            final,
            dma((18,)),
            dma((4,)),
            dma((4,)),
            dma((7,)),
            dma((7,)),
            dma((15,)),
            dma((15,)),
            dma((groups,)),
            dma((groups,)),
            dma((groups,)),
            dma((groups,)),
            dma((4,)),
            dma((4,)),
            dma((groups // 2,)),
            dma((groups // 2,)),
            dma((groups // 2,)),
            dma((groups // 2,)),
            dma((4,)),
            dma((4,)),
            dma((groups,)),
            dma((groups,)),
        ],
        compiler_params=pltpu.CompilerParams(
            collective_id=0, has_side_effects=True, vmem_limit_bytes=56 << 20
        ),
        name="layer",
    )(
        leaf_tokens.reshape(shard_rows, width),
        attn_gain.reshape(1, width),
        mlp_gain.reshape(1, width),
        jnp.transpose(prefix_owner),
        jnp.transpose(prefix_start),
        jnp.transpose(prefix_len),
        w_query,
        w_key,
        w_value,
        w_out,
        prefix_kv,
        jnp.transpose(expert_ids, (2, 1, 0)),
        jnp.transpose(gate_weights, (2, 1, 0)),
        request_of.reshape(1, requests),
        jnp.transpose(shared_in, (1, 2, 0)),
        shared_out,
        jnp.transpose(expert_in, (0, 2, 3, 1)),
        expert_out,
    )
    return mixed.reshape(requests, 1, width)


def solution(mesh):
    in_specs = (
        P(("dp", "tensor"), None, None),
        P(),
        P(None, "tensor"),
        P(None, "tensor"),
        P(None, "tensor"),
        P("tensor", None),
        P(None, "dp", "tensor"),
        P("dp", None),
        P("dp", None),
        P("dp", None),
        P(),
        P(None, None, "tensor"),
        P("tensor", None),
        P("dp", None, None, "tensor"),
        P("dp", "tensor", None),
        P("dp", None, None),
        P("dp", None, None),
        P("dp"),
    )
    out_specs = P("dp", "tensor", None)
    return jax.shard_map(
        on_device, mesh=mesh, in_specs=in_specs, out_specs=out_specs, check_vma=False
    )
```

time: 212 us -> 174 us (0.82)
  Pallas kernels: 195 us -> 170 us
  local copies, waits for them, and re-layouts: 12.8 us -> 1.47 us
  other arithmetic: 3.11 us -> 0 us
    pallas_call x2 -> x1, Pallas kernels: 195 us -> 170 us  [on_device(): pl.pallas_call(layer_kernel, out_shape=jax.ShapeDtypeStruct((requests, wi...]
    unnamed x21 -> x1, local copies, waits for them, and re-layouts: 9.07 us -> 1.47 us
where the time goes in v2:
time: 174 us; the launch traced here: 172 us
  Pallas kernels  170 us (98%)
    pallas_call x1, Pallas kernels, on_device(): pl.pallas_call(layer_kernel, out_shape=jax.ShapeDtypeStruct((requests, wi...  170 us

profile of v2, /device:TPU:32, one launch (start us, length us, event | category | flops | bytes accessed | tf_op | source)
XLA Modules:
  0.0 171.8 jit_solution(5663729359951256103)
XLA Ops:
  0.0 170.3 %layer.1 = bf16[16,2048]{1,0:T(8,128)(2,1)} custom-call(bf16[16,2048]{1,0:T(8,128)(2,1)} %bitcast.15, f32[1,2048]{1,0:T(1,128)} %bitcast.18, f32[1,2048]{1,0:T(1,128)} %bitcast.19, s32[3,16]{1,0:T(4,128)} %bitcast.20, s32[3,16]{1,0:T(4,128)} %bitcast.21, s32[3,16]{1,0:T(4,128)} %bitcast.22, bf16[2048,256]{1,0:T(8,128)(2,1)} %wq_hbm.1, ...), custom_call_target="tpu_custom_call" | custom-call | tf_op jit(solution)/shard_map/layer/pallas_call | solution.py:667
  170.3 1.5 copy.20

commit v3 on v2

--- a/solution.py
+++ b/solution.py
@@ -9,6 +9,7 @@
 EPS = 1e-06
 ROPE_BASE = 10000.0
 CAP = 16
+PARTS = 2
 MESH = pl.DeviceIdType.MESH
 BF = jnp.bfloat16
 F32 = jnp.float32
@@ -133,60 +134,76 @@
         copy.wait()
 
 
-def gather_column(p, buf, sems, between=None):
-    send, recv = sems
-    direct = []
-    for k in range(1, 4):
-        direct.append(
-            to_lane(buf.at[0, p.t], buf.at[0, p.t], send.at[k], recv.at[k], p.lane(k))
-        )
-        direct[-1].start()
-    for k in range(4):
-        direct.append(
-            to_both(
-                buf.at[0, p.t], buf.at[1, p.t], send.at[4 + k], recv.at[4 + k], p.mirror, p.lane(k)
-            )
-        )
-        direct[-1].start()
-    passed = [to_lane(buf.at[0, p.t], buf.at[0, p.t], send.at[0], recv.at[0], p.sib)]
-    passed[0].start()
-    if between is not None:
-        between()
-    for j in range(7):
-        origin, k = (0, j + 1) if j < 3 else (1, j - 3)
-        direct[j].wait_recv()
-        block = buf.at[origin, p.lane(4 - k)]
-        copy = to_lane(block, block, send.at[8 + j], recv.at[8 + j], p.sib)
-        copy.start()
-        passed.append(copy)
-    for copy in direct:
-        copy.wait_send()
-    for copy in passed:
-        copy.wait()
-
-
-def scatter_sum(p, part, sib_send, sib_recv, rs_send, rs_recv, sems):
-    send, recv = sems
-    for c in range(4):
-        sib_send[c] = part[:, c * 2 + (1 - p.core)].astype(BF)
-    swap = to_lane(sib_send, sib_recv, send.at[0], recv.at[0], p.sib)
-    swap.start()
-    swap.wait_recv()
-    copies = []
-    for k in range(1, 4):
-        there = lax.rem(p.chip + k, 4)
-        rs_send[k - 1] = (part[:, there * 2 + p.core] + sib_recv[there].astype(F32)).astype(BF)
-        copy = to_lane(rs_send.at[k - 1], rs_recv.at[k - 1], send.at[k], recv.at[k], p.lane(k))
-        copy.start()
-        copies.append(copy)
-    total = part[:, p.t] + sib_recv[p.chip].astype(F32)
-    for k in range(1, 4):
-        copies[k - 1].wait_recv()
-        total = total + rs_recv[k - 1].astype(F32)
-    swap.wait_send()
-    for copy in copies:
-        copy.wait_send()
-    return total
+class ColumnGather:
+    def __init__(self, p, buf, sems, s):
+        self.p, self.buf = p, buf.at[s]
+        send, recv = sems
+        self.send, self.recv = send.at[s], recv.at[s]
+        own, there = self.buf.at[0, p.t], self.buf.at[1, p.t]
+        self.direct = [
+            to_lane(own, own, self.send.at[k], self.recv.at[k], p.lane(k)) for k in range(1, 4)
+        ] + [
+            to_both(own, there, self.send.at[4 + k], self.recv.at[4 + k], p.mirror, p.lane(k))
+            for k in range(4)
+        ]
+        self.passed = [to_lane(own, own, self.send.at[0], self.recv.at[0], p.sib)]
+
+    def start(self):
+        for copy in self.direct + self.passed:
+            copy.start()
+
+    def finish(self):
+        p = self.p
+        for j in range(7):
+            origin, k = (0, j + 1) if j < 3 else (1, j - 3)
+            self.direct[j].wait_recv()
+            block = self.buf.at[origin, p.lane(4 - k)]
+            copy = to_lane(block, block, self.send.at[8 + j], self.recv.at[8 + j], p.sib)
+            copy.start()
+            self.passed.append(copy)
+        for copy in self.passed:
+            copy.wait_recv()
+
+    def drain(self):
+        for copy in self.direct + self.passed:
+            copy.wait_send()
+
+
+class ScatterSum:
+    def __init__(self, p, part, sib_send, sib_recv, rs_send, rs_recv, sems):
+        self.p, self.part = p, part
+        self.sib_send, self.sib_recv = sib_send, sib_recv
+        self.rs_send, self.rs_recv = rs_send, rs_recv
+        send, recv = sems
+        self.swap = to_lane(sib_send, sib_recv, send.at[0], recv.at[0], p.sib)
+        self.copies = [
+            to_lane(rs_send.at[k - 1], rs_recv.at[k - 1], send.at[k], recv.at[k], p.lane(k))
+            for k in range(1, 4)
+        ]
+
+    def start(self):
+        p = self.p
+        for c in range(4):
+            self.sib_send[c] = self.part[:, c * 2 + (1 - p.core)].astype(BF)
+        self.swap.start()
+        self.swap.wait_recv()
+        for k in range(1, 4):
+            there = lax.rem(p.chip + k, 4)
+            self.rs_send[k - 1] = (
+                self.part[:, there * 2 + p.core] + self.sib_recv[there].astype(F32)
+            ).astype(BF)
+            self.copies[k - 1].start()
+
+    def finish(self):
+        p = self.p
+        total = self.part[:, p.t] + self.sib_recv[p.chip].astype(F32)
+        for k in range(1, 4):
+            self.copies[k - 1].wait_recv()
+            total = total + self.rs_recv[k - 1].astype(F32)
+        self.swap.wait_send()
+        for copy in self.copies:
+            copy.wait_send()
+        return total
 
 
 def each(first, last, action):
@@ -202,11 +219,11 @@
     wo_hbm, kv_hbm, ids_hbm, gates_hbm, moves_hbm, shin_hbm, shout_hbm, ein_hbm, eout_hbm,
     out,
     leaf, gain1, gain2, owner, start, count, wq, wk, wv, wo, kv, ids, gates, moves, shin, shout,
-    win, wout, xg, qs, qr, bs, br, part1, sib_send1, sib_recv1, rs_send1, rs_recv1,
-    rows2, sb, xb, yb, zb, part2, sib_send2, sib_recv2, rs_send2, rs_recv2,
-    cross_send, cross_recv, fs, fr,
+    win, wout, xg, ms, mr, qs, qr, bs, br, part1, sib_send1, sib_recv1, rs_send1, rs_recv1,
+    rows2, sb, xb, hid, yb, zb, gate_hi, gate_lo, part2, sib_send2, sib_recv2, rs_send2, rs_recv2,
+    fs, fr,
     load_sem, swap_send, swap_recv, g1_send, g1_recv, g2_send, g2_recv,
-    q_send, q_recv, b_send, b_recv, r1_send, r1_recv,
+    m_send, m_recv, q_send, q_recv, b_send, b_recv, r1_send, r1_recv,
     d_send, d_recv, y_send, y_recv, r2_send, r2_recv, f_send, f_recv,
 ):
     p = Place()
@@ -239,7 +256,7 @@
             ("gain2", gain2_hbm, gain2),
             ("ids", ids_hbm, ids.at[0]),
             ("gates", gates_hbm, gates.at[0]),
-            ("moves", moves_hbm, moves),
+            ("moves", moves_hbm, moves.at[0]),
             ("shin", shin_hbm, shin),
             ("shout", shout_hbm, shout),
             ("ein", ein_hbm.at[p.core], win.at[:, pl.ds(0, units)]),
@@ -253,7 +270,6 @@
     loads["gain1"].wait()
     residual = leaf[...].astype(F32)
     xg[p.t] = rms_rows(residual, gain1[...])
-    await_all(p)
     swaps = [
         to_lane(
             ein_hbm.at[other], win.at[:, pl.ds(units, units)], swap_send.at[0], swap_recv.at[0], p.sib
@@ -263,6 +279,7 @@
         ),
         to_group(ids_hbm, ids.at[1], swap_send.at[2], swap_recv.at[2], p.mirror),
         to_group(gates_hbm, gates.at[1], swap_send.at[3], swap_recv.at[3], p.mirror),
+        to_group(moves_hbm, moves.at[1], swap_send.at[4], swap_recv.at[4], p.mirror),
     ]
 
     lane = iota((rows, HEAD_DIM), 1)
@@ -320,9 +337,19 @@
             meta = jnp.where(lane == 2, length_hi, meta)
             meta = jnp.where(lane == 1, begin - 32.0 * begin_hi, meta)
             metas.append(jnp.where(lane == 0, begin_hi, meta).astype(BF))
-        made["metas"] = metas
-
-    gather_rows(p, xg, (g1_send, g1_recv), tables)
+        ms[...] = nn_dot(made["places"], jnp.concatenate(metas, axis=0)).astype(BF).reshape(ms.shape)
+
+    def m_copy(k):
+        return to_group(ms.at[k], mr.at[k], m_send.at[k], m_recv.at[k], p.ahead(k))
+
+    tables()
+    await_all(p)
+
+    def ahead_of_queries():
+        each(1, groups, lambda k: m_copy(k).start())
+        mr[0] = ms[0]
+
+    gather_rows(p, xg, (g1_send, g1_recv), ahead_of_queries)
     for copy in swaps:
         copy.start()
     cosine, sine = made["cosine"], made["sine"]
@@ -337,9 +364,7 @@
     x = xg[...].reshape(rows, width)
     loads["wq"].wait()
     queries = rotated(nn_dot(x, wq[...]))
-    stacked = jnp.concatenate(
-        [jnp.concatenate([queries, meta], axis=1) for meta in made["metas"]], axis=0
-    )
+    stacked = jnp.concatenate([queries] * 3, axis=0)
     qs[...] = nn_dot(made["places"], stacked).astype(BF).reshape(qs.shape)
 
     def q_copy(k):
@@ -375,9 +400,10 @@
 
     def owner_chunk(c):
         first_k, last_k = jnp.maximum(c * per_chunk, 1), (c + 1) * per_chunk
+        each(first_k, last_k, lambda k: m_copy(k).wait_recv())
         each(first_k, last_k, lambda k: q_copy(k).wait_recv())
         block = qr[pl.ds(c * per_chunk, per_chunk)].reshape(chunk_rows, qs.shape[2])
-        meta = block[:, heads * HEAD_DIM :].astype(F32)
+        meta = mr[pl.ds(c * per_chunk, per_chunk)].reshape(chunk_rows, HEAD_DIM).astype(F32)
         first = meta[:, 0:1] * 32.0 + meta[:, 1:2]
         last = first + meta[:, 2:3] * 32.0 + meta[:, 3:4]
         visible = (key_id >= first) & (key_id < last)
@@ -396,7 +422,7 @@
             tail = jnp.where(chunk_lane == 2 * h + 1, log_part - log_hi, tail)
         pieces.append(tail.astype(BF))
         bs[pl.ds(c * per_chunk, per_chunk)] = jnp.concatenate(pieces, axis=1).reshape(
-            per_chunk, slot_rows, qs.shape[2]
+            per_chunk, slot_rows, bs.shape[2]
         )
         each(first_k, last_k, lambda k: b_copy(k).start())
 
@@ -407,7 +433,7 @@
         onehot(slot_lane == made["slot_cols"][:, level : level + 1]) for level in range(3)
     ]
     each(1, groups, lambda k: b_copy(k).wait_recv())
-    back_all = br[...].reshape(groups * slot_rows, qs.shape[2])
+    back_all = br[...].reshape(groups * slot_rows, br.shape[2])
     for level in range(3):
         back = nn_dot(picks[level], back_all)
         for h in range(heads):
@@ -426,10 +452,18 @@
 
     loads["wo"].wait()
     part1[...] = nn_dot(attended, wo[...]).reshape(part1.shape)
-    total = scatter_sum(p, part1, sib_send1, sib_recv1, rs_send1, rs_recv1, (r1_send, r1_recv))
-    residual_mid = residual + total[0]
+    summed = ScatterSum(
+        p, part1, sib_send1, sib_recv1, rs_send1, rs_recv1, (r1_send, r1_recv)
+    )
+    summed.start()
+    residual_mid = residual + summed.finish()[0]
     loads["gain2"].wait()
-    rows2[0, p.t] = rms_rows(residual_mid, gain2[...])
+    normed = rms_rows(residual_mid, gain2[...])
+    span = width // PARTS
+    gathers = [ColumnGather(p, rows2, (g2_send, g2_recv), s) for s in range(PARTS)]
+    for s in range(PARTS):
+        rows2[s, 0, p.t] = normed[:, s * span : (s + 1) * span]
+        gathers[s].start()
 
     tokens = 2 * rows
     wide_row = iota((tokens, tokens), 0)
@@ -484,47 +518,58 @@
             jnp.concatenate(slots + [gate_line, jnp.zeros((4, tokens), F32)], axis=0), (1, 0)
         )
 
-    gather_column(p, rows2, (g2_send, g2_recv), routing)
+    routing()
     turn = onehot(
         wide_col
         == wide_row // rows * rows
         + lax.rem(wide_row, requests) * leaf_len
         + lax.rem(wide_row, rows) // requests
     )
-    x = nn_dot(turn, rows2[...].reshape(tokens, width)).astype(BF)
-
-    cap = sb.shape[1]
+    cap = sb.shape[2]
     per_chunk2 = 4
     chunk2 = per_chunk2 * cap
-
-    def d_copy(k):
-        return to_group(sb.at[k], xb.at[k], d_send.at[k], d_recv.at[k], p.spot_ahead(k))
-
-    def y_copy(k):
-        return to_group(yb.at[k], zb.at[k], y_send.at[k], y_recv.at[k], p.spot_behind(k))
-
-    chunk_index = iota((chunk2, tokens), 0).astype(F32)
-
-    def pack(c):
-        where = chunk_index + (c * chunk2).astype(F32)
+    chunks2 = p.spots // per_chunk2
+
+    def d_copy(s, k):
+        return to_group(
+            sb.at[s, k], xb.at[s, k], d_send.at[s, k], d_recv.at[s, k], p.spot_ahead(k)
+        )
+
+    def y_copy(s, k):
+        return to_group(
+            yb.at[s, k], zb.at[s, k], y_send.at[s, k], y_recv.at[s, k], p.spot_behind(k)
+        )
+
+    chunk_index = iota((chunk2, tokens), 0)
+    picks = []
+    for c in range(chunks2):
+        where = (chunk_index + c * chunk2).astype(F32)
         pick = (where == routes["slots"][0]).astype(F32)
         for k in range(1, top_count):
             pick = pick + (where == routes["slots"][k]).astype(F32)
-        sb[pl.ds(c * per_chunk2, per_chunk2)] = (
-            nn_dot(pick.astype(BF), x).astype(BF).reshape(per_chunk2, cap, width)
-        )
-        each(
-            jnp.maximum(c * per_chunk2, 1), (c + 1) * per_chunk2, lambda k: d_copy(k).start()
-        )
-
-    each(0, p.spots // per_chunk2, pack)
-    xb[0] = sb[0]
+        picks.append(pick.astype(BF))
+    x_own = []
+    for s in range(PARTS):
+        gathers[s].finish()
+        x = nn_dot(turn, rows2[s].reshape(tokens, span)).astype(BF)
+        x_own.append(x[:rows])
+        for c in range(chunks2):
+            sb[s, c * per_chunk2 : (c + 1) * per_chunk2] = (
+                nn_dot(picks[c], x).astype(BF).reshape(per_chunk2, cap, span)
+            )
+            each(max(c * per_chunk2, 1), (c + 1) * per_chunk2, lambda k: d_copy(s, k).start())
+        xb[s, 0] = sb[s, 0]
 
     loads["shin"].wait()
     loads["shout"].wait()
-    x_own = x[:rows]
-    gate = nt_dot(x_own, shin[0])
-    up = nt_dot(x_own, shin[1])
+    def by_parts(pieces, weights):
+        total = nt_dot(pieces[0], weights[:, :span])
+        for s in range(1, PARTS):
+            total = total + nt_dot(pieces[s], weights[:, s * span : (s + 1) * span])
+        return total
+
+    gate = by_parts(x_own, shin.at[0])
+    up = by_parts(x_own, shin.at[1])
     hidden = (gate / (1.0 + jnp.exp(-gate)) * up).astype(BF)
     shared = nn_dot(hidden, shout[...])
     own_row = iota((rows, shard_rows), 0)
@@ -533,8 +578,21 @@
         lax.rem(own_row, requests) == (shard_rows // leaf_len) * p.t + own_col // leaf_len
     ) & (own_row // requests == lax.rem(own_col, leaf_len))
     shared = shared + exact_dot(mine.astype(F32), residual_mid)
-    part2[0] = shared.reshape(part2.shape[1:])
-    part2[1] = jnp.zeros(part2.shape[1:], F32)
+    for s in range(PARTS):
+        part2[s, 0] = shared[:, s * span : (s + 1) * span].reshape(part2.shape[2:])
+        part2[s, 1] = jnp.zeros(part2.shape[2:], F32)
+    all_slots = tokens * 2
+    token_lane = iota((tokens, all_slots), 1).astype(F32)
+    weights = jnp.zeros((tokens, all_slots), F32)
+    for k in range(top_count):
+        weights = weights + jnp.where(
+            token_lane == routes["cols"][:, k : k + 1],
+            routes["cols"][:, top_count + k : top_count + k + 1],
+            0.0,
+        )
+    high = weights.astype(BF)
+    gate_hi[...] = high
+    gate_lo[...] = (weights - high.astype(F32)).astype(BF)
 
     loads["ein"].wait()
     loads["eout"].wait()
@@ -543,54 +601,78 @@
 
     def compute(c):
         first_k, last_k = jnp.maximum(c * per_chunk2, 1), (c + 1) * per_chunk2
-        each(first_k, last_k, lambda k: d_copy(k).wait_recv())
-        block = xb[pl.ds(c * per_chunk2, per_chunk2)].reshape(chunk2, width)
-        gate_part = nt_dot(block, win[0])
-        up_part = nt_dot(block, win[1])
+        blocks = []
+        for s in range(PARTS):
+            each(first_k, last_k, lambda k: d_copy(s, k).wait_recv())
+            blocks.append(xb[s, pl.ds(c * per_chunk2, per_chunk2)].reshape(chunk2, span))
+        gate_part = by_parts(blocks, win.at[0])
+        up_part = by_parts(blocks, win.at[1])
         acted = (gate_part / (1.0 + jnp.exp(-gate_part)) * up_part).astype(BF)
-        yb[pl.ds(c * per_chunk2, per_chunk2)] = (
-            nn_dot(acted, wout[...]).astype(BF).reshape(per_chunk2, cap, width)
-        )
-        each(first_k, last_k, lambda k: y_copy(k).start())
-
-    each(0, p.spots // per_chunk2, compute)
-    zb[0] = yb[0]
-    token_lane = iota((tokens, chunk2), 1).astype(F32)
-
-    def combine(c):
-        first_k, last_k = jnp.maximum(c * per_chunk2, 1), (c + 1) * per_chunk2
-        each(first_k, last_k, lambda k: y_copy(k).wait_recv())
-        where = token_lane + (c * chunk2).astype(F32)
-        weights = jnp.zeros((tokens, chunk2), F32)
-        for k in range(top_count):
-            weights = weights + jnp.where(
-                where == routes["cols"][:, k : k + 1],
-                routes["cols"][:, top_count + k : top_count + k + 1],
-                0.0,
+        hid[c] = acted
+        yb[0, pl.ds(c * per_chunk2, per_chunk2)] = (
+            nn_dot(acted, wout[:, :span]).astype(BF).reshape(per_chunk2, cap, span)
+        )
+        each(first_k, last_k, lambda k: y_copy(0, k).start())
+
+    each(0, chunks2, compute)
+    zb[0, 0] = yb[0, 0]
+    for s in range(1, PARTS):
+
+        def later(c):
+            yb[s, pl.ds(c * per_chunk2, per_chunk2)] = (
+                nn_dot(hid[c], wout[:, s * span : (s + 1) * span])
+                .astype(BF)
+                .reshape(per_chunk2, cap, span)
             )
-        high = weights.astype(BF)
-        low = (weights - high.astype(F32)).astype(BF)
-        block = zb[pl.ds(c * per_chunk2, per_chunk2)].reshape(chunk2, width)
-        part2[...] += (nn_dot(high, block) + nn_dot(low, block)).reshape(part2.shape)
-
-    each(0, p.spots // per_chunk2, combine)
-    total = scatter_sum(p, part2, sib_send2, sib_recv2, rs_send2, rs_recv2, (r2_send, r2_recv))
-    cross_send[...] = total[1].astype(BF)
-    cross = to_group(cross_send, cross_recv, f_send.at[0], f_recv.at[0], p.mirror)
-    cross.start()
+            each(
+                jnp.maximum(c * per_chunk2, 1),
+                (c + 1) * per_chunk2,
+                lambda k: y_copy(s, k).start(),
+            )
+
+        each(0, chunks2, later)
+        zb[s, 0] = yb[s, 0]
+
+    sums = []
+    for s in range(PARTS):
+        for c in range(chunks2):
+            each(
+                max(c * per_chunk2, 1), (c + 1) * per_chunk2, lambda k: y_copy(s, k).wait_recv()
+            )
+            block = zb[s, c * per_chunk2 : (c + 1) * per_chunk2].reshape(chunk2, span)
+            cut = slice(c * chunk2, (c + 1) * chunk2)
+            part2[s] += (
+                nn_dot(gate_hi[:, cut], block) + nn_dot(gate_lo[:, cut], block)
+            ).reshape(part2.shape[1:])
+        sums.append(
+            ScatterSum(
+                p,
+                part2.at[s],
+                sib_send2.at[s],
+                sib_recv2.at[s],
+                rs_send2.at[s],
+                rs_recv2.at[s],
+                (r2_send.at[s], r2_recv.at[s]),
+            )
+        )
+        sums[s].start()
 
     loads["moves"].wait()
-    target = moves[...]
+    swaps[4].wait()
+    target = jnp.concatenate([moves[0], moves[1]], axis=1)
     aim = lax.rem(target // requests - p.me + groups, groups)
-    spot_tag = lax.rem(target, requests) + 1
-    goes = iota((groups, requests), 0) == aim
-    tags = jnp.sum(jnp.where(goes, spot_tag.astype(F32), 0.0), axis=1, keepdims=True)
-    cross.wait_recv()
-    mixed = (total[0] + cross_recv[...].astype(F32)).astype(BF)
-    outgoing = nn_dot(onehot(goes), mixed)
-    tagged = jnp.concatenate([outgoing, jnp.broadcast_to(tags, (groups, 128))], axis=1)
+    spot_tag = (lax.rem(target, requests) + 1).astype(F32)
+    pairs = (2 * groups, 2 * requests)
+    goes = (iota(pairs, 0) // 2 == aim) & (lax.rem(iota(pairs, 0), 2) == iota(pairs, 1) // requests)
+    tags = jnp.sum(jnp.where(goes, spot_tag, 0.0), axis=1, keepdims=True)
+    goes = onehot(goes)
+    pieces = []
+    for s in range(PARTS):
+        mixed = sums[s].finish().astype(BF).reshape(2 * requests, span)
+        pieces.append(nn_dot(goes, mixed))
+    tagged = jnp.concatenate(pieces + [jnp.broadcast_to(tags, (2 * groups, 128))], axis=1)
     for k in range(groups):
-        fs[k] = tagged[k : k + 1]
+        fs[k] = tagged[2 * k : 2 * k + 2].astype(BF)
 
     def f_copy(k):
         return to_group(fs.at[k], fr.at[k], f_send.at[k], f_recv.at[k], p.ahead(k))
@@ -598,8 +680,8 @@
     each(1, groups, lambda k: f_copy(k).start())
     fr[0] = fs[0]
     each(1, groups, lambda k: f_copy(k).wait_recv())
-    landed = jnp.concatenate([fr[k] for k in range(groups)], axis=0)
-    place_lane = iota((groups, requests), 1).astype(F32) + 1.0
+    landed = jnp.concatenate([fr[k].astype(F32) for k in range(groups)], axis=0)
+    place_lane = iota((2 * groups, requests), 1).astype(F32) + 1.0
     settle = onehot(landed[:, width : width + 1] == place_lane)
     out[...] = lax.dot_general(
         settle,
@@ -608,16 +690,19 @@
         preferred_element_type=F32,
     ).astype(BF)
 
-    cross.wait_send()
+    for gather in gathers:
+        gather.drain()
 
     def sent(k):
+        m_copy(k).wait_send()
         q_copy(k).wait_send()
         b_copy(k).wait_send()
         f_copy(k).wait_send()
 
     def sent2(k):
-        d_copy(k).wait_send()
-        y_copy(k).wait_send()
+        for s in range(PARTS):
+            d_copy(s, k).wait_send()
+            y_copy(s, k).wait_send()
 
     each(1, groups, sent)
     each(1, p.spots, sent2)
@@ -656,13 +741,18 @@
     hbm = pl.BlockSpec(memory_space=pltpu.HBM)
     dma = pltpu.SemaphoreType.DMA
     vm = pltpu.VMEM
-    exchange = vm((groups, slot_rows, payload), BF)
+    meta = vm((groups, slot_rows, 128), BF)
+    exchange = vm((groups, slot_rows, local_width), BF)
+    answer = vm((groups, slot_rows, payload), BF)
     table = vm((3, requests), jnp.int32)
     weight = vm(w_query.shape, BF)
     block1 = vm((4, 1, shard_rows, width), BF)
-    block2 = vm((4, 2, shard_rows, width), BF)
-    rows_in = vm((groups // 2, 2 * CAP, width), BF)
-    final = vm((groups, 1, width + 128), F32)
+    span = width // PARTS
+    tokens = 2 * lanes * shard_rows
+    block2 = vm((PARTS, 4, 2, shard_rows, span), BF)
+    rows_in = vm((PARTS, groups // 2, 2 * CAP, span), BF)
+    gate_table = vm((tokens, groups // 2 * 2 * CAP), BF)
+    final = vm((groups, 2, width + 128), BF)
     column = (2, top_count, leaf_len, requests)
     mixed = pl.pallas_call(
         layer_kernel,
@@ -683,54 +773,59 @@
             vm(prefix_kv.shape, BF),
             vm(column, jnp.int32),
             vm(column, F32),
-            vm((1, requests), jnp.int32),
+            vm((2, 1, requests), jnp.int32),
             vm((2, units, width), BF),
             vm((units, width), BF),
             vm((2, 2 * units, width), BF),
             vm((2 * units, width), BF),
             vm((lanes, shard_rows, width), BF),
+            meta,
+            meta,
             exchange,
             exchange,
-            exchange,
-            exchange,
+            answer,
+            answer,
             vm((1, lanes, shard_rows, width), F32),
             block1,
             block1,
             block1,
             block1,
-            vm((2, lanes, shard_rows, width), BF),
+            vm((PARTS, 2, lanes, shard_rows, span), BF),
             rows_in,
             rows_in,
+            vm((4, groups // 8 * 2 * CAP, 2 * units), BF),
             rows_in,
             rows_in,
-            vm((2, lanes, shard_rows, width), F32),
+            gate_table,
+            gate_table,
+            vm((PARTS, 2, lanes, shard_rows, span), F32),
             block2,
             block2,
             block2,
             block2,
-            vm((shard_rows, width), BF),
-            vm((shard_rows, width), BF),
             final,
             final,
             dma((18,)),
-            dma((4,)),
-            dma((4,)),
+            dma((5,)),
+            dma((5,)),
             dma((7,)),
             dma((7,)),
-            dma((15,)),
-            dma((15,)),
+            dma((PARTS, 15)),
+            dma((PARTS, 15)),
+            dma((groups,)),
+            dma((groups,)),
             dma((groups,)),
             dma((groups,)),
             dma((groups,)),
             dma((groups,)),
             dma((4,)),
             dma((4,)),
-            dma((groups // 2,)),
-            dma((groups // 2,)),
-            dma((groups // 2,)),
-            dma((groups // 2,)),
-            dma((4,)),
-            dma((4,)),
+            dma((PARTS, groups // 2)),
+            dma((PARTS, groups // 2)),
+            dma((PARTS, groups // 2)),
+            dma((PARTS, groups // 2)),
+            dma((PARTS, 4)),
+            dma((PARTS, 4)),
             dma((groups,)),
             dma((groups,)),
         ],

time: 174 us -> 158 us (0.908); the launches traced: 172 us -> 158 us
  Pallas kernels: 170 us -> 157 us
    pallas_call x1, Pallas kernels: 170 us -> 157 us  [on_device(): pl.pallas_call(layer_kernel, out_shape=jax.ShapeDtypeStruct((requests, wi...]
where the time goes in v3:
time: 158 us
  Pallas kernels  157 us (99%)
    pallas_call x1, Pallas kernels, on_device(): pl.pallas_call(layer_kernel, out_shape=jax.ShapeDtypeStruct((requests, wi...  157 us

profile of v3, /device:TPU:32, one launch (start us, length us, event | category | flops | bytes accessed | tf_op | source)
XLA Modules:
  0.0 158.0 jit_solution(15024015117347816808)
XLA Ops:
  0.0 156.6 %layer.1 = bf16[16,2048]{1,0:T(8,128)(2,1)} custom-call(bf16[16,2048]{1,0:T(8,128)(2,1)} %bitcast.15, f32[1,2048]{1,0:T(1,128)} %bitcast.18, f32[1,2048]{1,0:T(1,128)} %bitcast.19, s32[3,16]{1,0:T(4,128)} %bitcast.20, s32[3,16]{1,0:T(4,128)} %bitcast.21, s32[3,16]{1,0:T(4,128)} %bitcast.22, bf16[2048,256]{1,0:T(8,128)(2,1)} %wq_hbm.1, ...), custom_call_target="tpu_custom_call" | custom-call | tf_op jit(solution)/shard_map/layer/pallas_call | solution.py:757
  156.6 1.5 copy.20

commit v4 on v3

--- a/solution.py
+++ b/solution.py
@@ -9,7 +9,8 @@
 EPS = 1e-06
 ROPE_BASE = 10000.0
 CAP = 16
-PARTS = 2
+PARTS = 4
+FINAL = ((0, 1, 2), (3,))
 MESH = pl.DeviceIdType.MESH
 BF = jnp.bfloat16
 F32 = jnp.float32
@@ -219,14 +220,15 @@
     wo_hbm, kv_hbm, ids_hbm, gates_hbm, moves_hbm, shin_hbm, shout_hbm, ein_hbm, eout_hbm,
     out,
     leaf, gain1, gain2, owner, start, count, wq, wk, wv, wo, kv, ids, gates, moves, shin, shout,
-    win, wout, xg, ms, mr, qs, qr, bs, br, part1, sib_send1, sib_recv1, rs_send1, rs_recv1,
+    win, wout, xg, qs, qr, bs, br, part1, sib_send1, sib_recv1, rs_send1, rs_recv1,
     rows2, sb, xb, hid, yb, zb, gate_hi, gate_lo, part2, sib_send2, sib_recv2, rs_send2, rs_recv2,
-    fs, fr,
+    fs0, fs1, fr0, fr1,
     load_sem, swap_send, swap_recv, g1_send, g1_recv, g2_send, g2_recv,
-    m_send, m_recv, q_send, q_recv, b_send, b_recv, r1_send, r1_recv,
+    q_send, q_recv, b_send, b_recv, r1_send, r1_recv,
     d_send, d_recv, y_send, y_recv, r2_send, r2_recv, f_send, f_recv,
 ):
     p = Place()
+    fs, fr = (fs0, fs1), (fr0, fr1)
     groups = p.groups
     lanes, shard_rows, width = xg.shape
     rows = lanes * shard_rows
@@ -337,19 +339,11 @@
             meta = jnp.where(lane == 2, length_hi, meta)
             meta = jnp.where(lane == 1, begin - 32.0 * begin_hi, meta)
             metas.append(jnp.where(lane == 0, begin_hi, meta).astype(BF))
-        ms[...] = nn_dot(made["places"], jnp.concatenate(metas, axis=0)).astype(BF).reshape(ms.shape)
-
-    def m_copy(k):
-        return to_group(ms.at[k], mr.at[k], m_send.at[k], m_recv.at[k], p.ahead(k))
+        made["metas"] = metas
 
     tables()
     await_all(p)
-
-    def ahead_of_queries():
-        each(1, groups, lambda k: m_copy(k).start())
-        mr[0] = ms[0]
-
-    gather_rows(p, xg, (g1_send, g1_recv), ahead_of_queries)
+    gather_rows(p, xg, (g1_send, g1_recv))
     for copy in swaps:
         copy.start()
     cosine, sine = made["cosine"], made["sine"]
@@ -364,7 +358,9 @@
     x = xg[...].reshape(rows, width)
     loads["wq"].wait()
     queries = rotated(nn_dot(x, wq[...]))
-    stacked = jnp.concatenate([queries] * 3, axis=0)
+    stacked = jnp.concatenate(
+        [jnp.concatenate([queries, meta], axis=1) for meta in made["metas"]], axis=0
+    )
     qs[...] = nn_dot(made["places"], stacked).astype(BF).reshape(qs.shape)
 
     def q_copy(k):
@@ -400,10 +396,9 @@
 
     def owner_chunk(c):
         first_k, last_k = jnp.maximum(c * per_chunk, 1), (c + 1) * per_chunk
-        each(first_k, last_k, lambda k: m_copy(k).wait_recv())
         each(first_k, last_k, lambda k: q_copy(k).wait_recv())
         block = qr[pl.ds(c * per_chunk, per_chunk)].reshape(chunk_rows, qs.shape[2])
-        meta = mr[pl.ds(c * per_chunk, per_chunk)].reshape(chunk_rows, HEAD_DIM).astype(F32)
+        meta = block[:, heads * HEAD_DIM :].astype(F32)
         first = meta[:, 0:1] * 32.0 + meta[:, 1:2]
         last = first + meta[:, 2:3] * 32.0 + meta[:, 3:4]
         visible = (key_id >= first) & (key_id < last)
@@ -432,39 +427,6 @@
     picks = [
         onehot(slot_lane == made["slot_cols"][:, level : level + 1]) for level in range(3)
     ]
-    each(1, groups, lambda k: b_copy(k).wait_recv())
-    back_all = br[...].reshape(groups * slot_rows, br.shape[2])
-    for level in range(3):
-        back = nn_dot(picks[level], back_all)
-        for h in range(heads):
-            base = heads * HEAD_DIM + 2 * h
-            outs[h].append(back[:, h * HEAD_DIM : (h + 1) * HEAD_DIM])
-            logs[h].append(back[:, base : base + 1] + back[:, base + 1 : base + 2])
-    merged = []
-    for h in range(heads):
-        top = jnp.maximum(jnp.maximum(logs[h][0], logs[h][1]), jnp.maximum(logs[h][2], logs[h][3]))
-        scales = [jnp.exp(one - top) for one in logs[h]]
-        weighted = scales[0] * outs[h][0]
-        for j in range(1, 4):
-            weighted = weighted + scales[j] * outs[h][j]
-        merged.append(weighted / (scales[0] + scales[1] + scales[2] + scales[3]))
-    attended = jnp.concatenate(merged, axis=1).astype(BF)
-
-    loads["wo"].wait()
-    part1[...] = nn_dot(attended, wo[...]).reshape(part1.shape)
-    summed = ScatterSum(
-        p, part1, sib_send1, sib_recv1, rs_send1, rs_recv1, (r1_send, r1_recv)
-    )
-    summed.start()
-    residual_mid = residual + summed.finish()[0]
-    loads["gain2"].wait()
-    normed = rms_rows(residual_mid, gain2[...])
-    span = width // PARTS
-    gathers = [ColumnGather(p, rows2, (g2_send, g2_recv), s) for s in range(PARTS)]
-    for s in range(PARTS):
-        rows2[s, 0, p.t] = normed[:, s * span : (s + 1) * span]
-        gathers[s].start()
-
     tokens = 2 * rows
     wide_row = iota((tokens, tokens), 0)
     wide_col = iota((tokens, tokens), 1)
@@ -530,24 +492,57 @@
     chunk2 = per_chunk2 * cap
     chunks2 = p.spots // per_chunk2
 
-    def d_copy(s, k):
-        return to_group(
-            sb.at[s, k], xb.at[s, k], d_send.at[s, k], d_recv.at[s, k], p.spot_ahead(k)
-        )
-
-    def y_copy(s, k):
-        return to_group(
-            yb.at[s, k], zb.at[s, k], y_send.at[s, k], y_recv.at[s, k], p.spot_behind(k)
-        )
-
     chunk_index = iota((chunk2, tokens), 0)
-    picks = []
+    row_picks = []
     for c in range(chunks2):
         where = (chunk_index + c * chunk2).astype(F32)
         pick = (where == routes["slots"][0]).astype(F32)
         for k in range(1, top_count):
             pick = pick + (where == routes["slots"][k]).astype(F32)
-        picks.append(pick.astype(BF))
+        row_picks.append(pick.astype(BF))
+    each(1, groups, lambda k: b_copy(k).wait_recv())
+    back_all = br[...].reshape(groups * slot_rows, br.shape[2])
+    for level in range(3):
+        back = nn_dot(picks[level], back_all)
+        for h in range(heads):
+            base = heads * HEAD_DIM + 2 * h
+            outs[h].append(back[:, h * HEAD_DIM : (h + 1) * HEAD_DIM])
+            logs[h].append(back[:, base : base + 1] + back[:, base + 1 : base + 2])
+    merged = []
+    for h in range(heads):
+        top = jnp.maximum(jnp.maximum(logs[h][0], logs[h][1]), jnp.maximum(logs[h][2], logs[h][3]))
+        scales = [jnp.exp(one - top) for one in logs[h]]
+        weighted = scales[0] * outs[h][0]
+        for j in range(1, 4):
+            weighted = weighted + scales[j] * outs[h][j]
+        merged.append(weighted / (scales[0] + scales[1] + scales[2] + scales[3]))
+    attended = jnp.concatenate(merged, axis=1).astype(BF)
+
+    loads["wo"].wait()
+    part1[...] = nn_dot(attended, wo[...]).reshape(part1.shape)
+    summed = ScatterSum(
+        p, part1, sib_send1, sib_recv1, rs_send1, rs_recv1, (r1_send, r1_recv)
+    )
+    summed.start()
+    residual_mid = residual + summed.finish()[0]
+    loads["gain2"].wait()
+    normed = rms_rows(residual_mid, gain2[...])
+    span = width // PARTS
+    gathers = [ColumnGather(p, rows2, (g2_send, g2_recv), s) for s in range(PARTS)]
+    for s in range(PARTS):
+        rows2[s, 0, p.t] = normed[:, s * span : (s + 1) * span]
+        gathers[s].start()
+
+    def d_copy(s, k):
+        return to_group(
+            sb.at[s, k], xb.at[s, k], d_send.at[s, k], d_recv.at[s, k], p.spot_ahead(k)
+        )
+
+    def y_copy(s, k):
+        return to_group(
+            yb.at[s, k], zb.at[s, k], y_send.at[s, k], y_recv.at[s, k], p.spot_behind(k)
+        )
+
     x_own = []
     for s in range(PARTS):
         gathers[s].finish()
@@ -555,7 +550,7 @@
         x_own.append(x[:rows])
         for c in range(chunks2):
             sb[s, c * per_chunk2 : (c + 1) * per_chunk2] = (
-                nn_dot(picks[c], x).astype(BF).reshape(per_chunk2, cap, span)
+                nn_dot(row_picks[c], x).astype(BF).reshape(per_chunk2, cap, span)
             )
             each(max(c * per_chunk2, 1), (c + 1) * per_chunk2, lambda k: d_copy(s, k).start())
         xb[s, 0] = sb[s, 0]
@@ -614,6 +609,13 @@
         )
         each(first_k, last_k, lambda k: y_copy(0, k).start())
 
+    def sent(k):
+        q_copy(k).wait_send()
+        b_copy(k).wait_send()
+
+    for gather in gathers:
+        gather.drain()
+    each(1, groups, sent)
     each(0, chunks2, compute)
     zb[0, 0] = yb[0, 0]
     for s in range(1, PARTS):
@@ -633,30 +635,6 @@
         each(0, chunks2, later)
         zb[s, 0] = yb[s, 0]
 
-    sums = []
-    for s in range(PARTS):
-        for c in range(chunks2):
-            each(
-                max(c * per_chunk2, 1), (c + 1) * per_chunk2, lambda k: y_copy(s, k).wait_recv()
-            )
-            block = zb[s, c * per_chunk2 : (c + 1) * per_chunk2].reshape(chunk2, span)
-            cut = slice(c * chunk2, (c + 1) * chunk2)
-            part2[s] += (
-                nn_dot(gate_hi[:, cut], block) + nn_dot(gate_lo[:, cut], block)
-            ).reshape(part2.shape[1:])
-        sums.append(
-            ScatterSum(
-                p,
-                part2.at[s],
-                sib_send2.at[s],
-                sib_recv2.at[s],
-                rs_send2.at[s],
-                rs_recv2.at[s],
-                (r2_send.at[s], r2_recv.at[s]),
-            )
-        )
-        sums[s].start()
-
     loads["moves"].wait()
     swaps[4].wait()
     target = jnp.concatenate([moves[0], moves[1]], axis=1)
@@ -665,47 +643,76 @@
     pairs = (2 * groups, 2 * requests)
     goes = (iota(pairs, 0) // 2 == aim) & (lax.rem(iota(pairs, 0), 2) == iota(pairs, 1) // requests)
     tags = jnp.sum(jnp.where(goes, spot_tag, 0.0), axis=1, keepdims=True)
+    tags = jnp.broadcast_to(tags, (2 * groups, 128))
     goes = onehot(goes)
-    pieces = []
-    for s in range(PARTS):
-        mixed = sums[s].finish().astype(BF).reshape(2 * requests, span)
-        pieces.append(nn_dot(goes, mixed))
-    tagged = jnp.concatenate(pieces + [jnp.broadcast_to(tags, (2 * groups, 128))], axis=1)
-    for k in range(groups):
-        fs[k] = tagged[2 * k : 2 * k + 2].astype(BF)
-
-    def f_copy(k):
-        return to_group(fs.at[k], fr.at[k], f_send.at[k], f_recv.at[k], p.ahead(k))
-
-    each(1, groups, lambda k: f_copy(k).start())
-    fr[0] = fs[0]
-    each(1, groups, lambda k: f_copy(k).wait_recv())
-    landed = jnp.concatenate([fr[k].astype(F32) for k in range(groups)], axis=0)
-    place_lane = iota((2 * groups, requests), 1).astype(F32) + 1.0
-    settle = onehot(landed[:, width : width + 1] == place_lane)
-    out[...] = lax.dot_general(
-        settle,
-        landed[:, :width].astype(BF),
-        (((0,), (0,)), ((), ())),
-        preferred_element_type=F32,
-    ).astype(BF)
-
-    for gather in gathers:
-        gather.drain()
-
-    def sent(k):
-        m_copy(k).wait_send()
-        q_copy(k).wait_send()
-        b_copy(k).wait_send()
-        f_copy(k).wait_send()
+
+    def f_copy(j, k):
+        return to_group(
+            fs[j].at[k], fr[j].at[k], f_send.at[j, k], f_recv.at[j, k], p.ahead(k)
+        )
+
+    sums = []
+    for j, members in enumerate(FINAL):
+        for s in members:
+            for c in range(chunks2):
+                each(
+                    max(c * per_chunk2, 1),
+                    (c + 1) * per_chunk2,
+                    lambda k: y_copy(s, k).wait_recv(),
+                )
+                block = zb[s, c * per_chunk2 : (c + 1) * per_chunk2].reshape(chunk2, span)
+                cut = slice(c * chunk2, (c + 1) * chunk2)
+                part2[s] += (
+                    nn_dot(gate_hi[:, cut], block) + nn_dot(gate_lo[:, cut], block)
+                ).reshape(part2.shape[1:])
+            sums.append(
+                ScatterSum(
+                    p,
+                    part2.at[s],
+                    sib_send2.at[s],
+                    sib_recv2.at[s],
+                    rs_send2.at[s],
+                    rs_recv2.at[s],
+                    (r2_send.at[s], r2_recv.at[s]),
+                )
+            )
+            sums[s].start()
+        pieces = []
+        for s in members:
+            mixed = sums[s].finish().astype(BF).reshape(2 * requests, span)
+            pieces.append(nn_dot(goes, mixed))
+        if j == 0:
+            pieces.append(tags)
+        outgoing = jnp.concatenate(pieces, axis=1)
+        for k in range(groups):
+            fs[j][k] = outgoing[2 * k : 2 * k + 2].astype(BF)
+        each(1, groups, lambda k: f_copy(j, k).start())
+        fr[j][0] = fs[j][0]
 
     def sent2(k):
         for s in range(PARTS):
             d_copy(s, k).wait_send()
             y_copy(s, k).wait_send()
 
-    each(1, groups, sent)
     each(1, p.spots, sent2)
+    settle = None
+    base = 0
+    for j, members in enumerate(FINAL):
+        each(1, groups, lambda k: f_copy(j, k).wait_recv())
+        landed = jnp.concatenate([fr[j][k].astype(F32) for k in range(groups)], axis=0)
+        wide = len(members) * span
+        if j == 0:
+            place_lane = iota((2 * groups, requests), 1).astype(F32) + 1.0
+            settle = onehot(landed[:, wide : wide + 1] == place_lane)
+        out[:, base : base + wide] = lax.dot_general(
+            settle,
+            landed[:, :wide].astype(BF),
+            (((0,), (0,)), ((), ())),
+            preferred_element_type=F32,
+        ).astype(BF)
+        base += wide
+    for j in range(len(FINAL)):
+        each(1, groups, lambda k: f_copy(j, k).wait_send())
 
 
 def on_device(
@@ -741,9 +748,7 @@
     hbm = pl.BlockSpec(memory_space=pltpu.HBM)
     dma = pltpu.SemaphoreType.DMA
     vm = pltpu.VMEM
-    meta = vm((groups, slot_rows, 128), BF)
-    exchange = vm((groups, slot_rows, local_width), BF)
-    answer = vm((groups, slot_rows, payload), BF)
+    exchange = vm((groups, slot_rows, payload), BF)
     table = vm((3, requests), jnp.int32)
     weight = vm(w_query.shape, BF)
     block1 = vm((4, 1, shard_rows, width), BF)
@@ -752,7 +757,8 @@
     block2 = vm((PARTS, 4, 2, shard_rows, span), BF)
     rows_in = vm((PARTS, groups // 2, 2 * CAP, span), BF)
     gate_table = vm((tokens, groups // 2 * 2 * CAP), BF)
-    final = vm((groups, 2, width + 128), BF)
+    final0 = vm((groups, 2, len(FINAL[0]) * span + 128), BF)
+    final1 = vm((groups, 2, len(FINAL[1]) * span), BF)
     column = (2, top_count, leaf_len, requests)
     mixed = pl.pallas_call(
         layer_kernel,
@@ -779,12 +785,10 @@
             vm((2, 2 * units, width), BF),
             vm((2 * units, width), BF),
             vm((lanes, shard_rows, width), BF),
-            meta,
-            meta,
             exchange,
             exchange,
-            answer,
-            answer,
+            exchange,
+            exchange,
             vm((1, lanes, shard_rows, width), F32),
             block1,
             block1,
@@ -803,8 +807,10 @@
             block2,
             block2,
             block2,
-            final,
-            final,
+            final0,
+            final1,
+            final0,
+            final1,
             dma((18,)),
             dma((5,)),
             dma((5,)),
@@ -812,8 +818,6 @@
             dma((7,)),
             dma((PARTS, 15)),
             dma((PARTS, 15)),
-            dma((groups,)),
-            dma((groups,)),
             dma((groups,)),
             dma((groups,)),
             dma((groups,)),
@@ -826,8 +830,8 @@
             dma((PARTS, groups // 2)),
             dma((PARTS, 4)),
             dma((PARTS, 4)),
-            dma((groups,)),
-            dma((groups,)),
+            dma((2, groups)),
+            dma((2, groups)),
         ],
         compiler_params=pltpu.CompilerParams(
             collective_id=0, has_side_effects=True, vmem_limit_bytes=56 << 20

time: 158 us -> 148 us (0.937); the launches traced: 158 us -> 146 us
  Pallas kernels: 157 us -> 145 us
    pallas_call x1, Pallas kernels: 157 us -> 145 us  [on_device(): pl.pallas_call(layer_kernel, out_shape=jax.ShapeDtypeStruct((requests, wi...]
where the time goes in v4:
time: 148 us; the launch traced here: 146 us
  Pallas kernels  145 us (98%)
    pallas_call x1, Pallas kernels, on_device(): pl.pallas_call(layer_kernel, out_shape=jax.ShapeDtypeStruct((requests, wi...  145 us

profile of v4, /device:TPU:32, one launch (start us, length us, event | category | flops | bytes accessed | tf_op | source)
XLA Modules:
  0.0 146.2 jit_solution(14817376210185542589)
XLA Ops:
  0.0 144.7 %layer.1 = bf16[16,2048]{1,0:T(8,128)(2,1)} custom-call(bf16[16,2048]{1,0:T(8,128)(2,1)} %bitcast.15, f32[1,2048]{1,0:T(1,128)} %bitcast.18, f32[1,2048]{1,0:T(1,128)} %bitcast.19, s32[3,16]{1,0:T(4,128)} %bitcast.20, s32[3,16]{1,0:T(4,128)} %bitcast.21, s32[3,16]{1,0:T(4,128)} %bitcast.22, bf16[2048,256]{1,0:T(8,128)(2,1)} %wq_hbm.1, ...), custom_call_target="tpu_custom_call" | custom-call | tf_op jit(solution)/shard_map/layer/pallas_call | solution.py:763
  144.8 1.5 %copy.20 = bf16[16,1,2048]{2,0,1:T(8,128)(2,1)} copy(bf16[16,1,2048]{2,0,1:T(8,128)(2,1)} %bitcast.14) | data formatting | bytes 131072

commit v5 on v4

--- a/solution.py
+++ b/solution.py
@@ -11,6 +11,8 @@
 CAP = 16
 PARTS = 4
 FINAL = ((0, 1, 2), (3,))
+CHUNK = 4
+OWNERS = 16
 MESH = pl.DeviceIdType.MESH
 BF = jnp.bfloat16
 F32 = jnp.float32
@@ -221,7 +223,7 @@
     out,
     leaf, gain1, gain2, owner, start, count, wq, wk, wv, wo, kv, ids, gates, moves, shin, shout,
     win, wout, xg, qs, qr, bs, br, part1, sib_send1, sib_recv1, rs_send1, rs_recv1,
-    rows2, sb, xb, hid, yb, zb, gate_hi, gate_lo, part2, sib_send2, sib_recv2, rs_send2, rs_recv2,
+    rows2, sb, xb, hid, gate_sum, up_sum, yb, zb, gate_hi, gate_lo, part2, sib_send2, sib_recv2, rs_send2, rs_recv2,
     fs0, fs1, fr0, fr1,
     load_sem, swap_send, swap_recv, g1_send, g1_recv, g2_send, g2_recv,
     q_send, q_recv, b_send, b_recv, r1_send, r1_recv,
@@ -389,7 +391,7 @@
         logs[h].append(top + jnp.log(total))
 
     loads["kv"].wait()
-    per_chunk = 8
+    per_chunk = OWNERS
     chunk_rows = per_chunk * slot_rows
     key_id = iota((chunk_rows, keys), 1).astype(F32)
     chunk_lane = iota((chunk_rows, HEAD_DIM), 1)
@@ -488,7 +490,7 @@
         + lax.rem(wide_row, rows) // requests
     )
     cap = sb.shape[2]
-    per_chunk2 = 4
+    per_chunk2 = CHUNK
     chunk2 = per_chunk2 * cap
     chunks2 = p.spots // per_chunk2
 
@@ -594,14 +596,36 @@
     swaps[0].wait()
     swaps[1].wait()
 
+    def product(s, c, weights):
+        block = xb[s, pl.ds(c * per_chunk2, per_chunk2)].reshape(chunk2, span)
+        return nt_dot(block, weights[:, s * span : (s + 1) * span])
+
+    def arrived(s, c):
+        each(
+            jnp.maximum(c * per_chunk2, 1),
+            (c + 1) * per_chunk2,
+            lambda k: d_copy(s, k).wait_recv(),
+        )
+
+    for s in range(PARTS - 1):
+
+        def gather_products(c):
+            arrived(s, c)
+            gate_part = product(s, c, win.at[0])
+            up_part = product(s, c, win.at[1])
+            if s:
+                gate_part = gate_part + gate_sum[c]
+                up_part = up_part + up_sum[c]
+            gate_sum[c] = gate_part
+            up_sum[c] = up_part
+
+        each(0, chunks2, gather_products)
+
     def compute(c):
         first_k, last_k = jnp.maximum(c * per_chunk2, 1), (c + 1) * per_chunk2
-        blocks = []
-        for s in range(PARTS):
-            each(first_k, last_k, lambda k: d_copy(s, k).wait_recv())
-            blocks.append(xb[s, pl.ds(c * per_chunk2, per_chunk2)].reshape(chunk2, span))
-        gate_part = by_parts(blocks, win.at[0])
-        up_part = by_parts(blocks, win.at[1])
+        arrived(PARTS - 1, c)
+        gate_part = gate_sum[c] + product(PARTS - 1, c, win.at[0])
+        up_part = up_sum[c] + product(PARTS - 1, c, win.at[1])
         acted = (gate_part / (1.0 + jnp.exp(-gate_part)) * up_part).astype(BF)
         hid[c] = acted
         yb[0, pl.ds(c * per_chunk2, per_chunk2)] = (
@@ -756,6 +780,7 @@
     tokens = 2 * lanes * shard_rows
     block2 = vm((PARTS, 4, 2, shard_rows, span), BF)
     rows_in = vm((PARTS, groups // 2, 2 * CAP, span), BF)
+    chunked = (groups // 2 // CHUNK, CHUNK * 2 * CAP, 2 * units)
     gate_table = vm((tokens, groups // 2 * 2 * CAP), BF)
     final0 = vm((groups, 2, len(FINAL[0]) * span + 128), BF)
     final1 = vm((groups, 2, len(FINAL[1]) * span), BF)
@@ -797,7 +822,9 @@
             vm((PARTS, 2, lanes, shard_rows, span), BF),
             rows_in,
             rows_in,
-            vm((4, groups // 8 * 2 * CAP, 2 * units), BF),
+            vm(chunked, BF),
+            vm(chunked, F32),
+            vm(chunked, F32),
             rows_in,
             rows_in,
             gate_table,

time: 148 us -> 145 us (0.980)
  Pallas kernels: 145 us -> 143 us
    pallas_call x1, Pallas kernels: 145 us -> 143 us  [on_device(): pl.pallas_call(layer_kernel, out_shape=jax.ShapeDtypeStruct((requests, wi...]
where the time goes in v5:
time: 145 us; the launch traced here: 144 us
  Pallas kernels  143 us (99%)
  local copies, waits for them, and re-layouts  1.47 us (1%)
    pallas_call x1, Pallas kernels, on_device(): pl.pallas_call(layer_kernel, out_shape=jax.ShapeDtypeStruct((requests, wi...  143 us

profile of v5, /device:TPU:32, one launch (start us, length us, event | category | flops | bytes accessed | tf_op | source)
XLA Modules:
  0.0 144.0 jit_solution(14948202632038053348)
XLA Ops:
  0.0 142.5 %layer.1 = bf16[16,2048]{1,0:T(8,128)(2,1)} custom-call(bf16[16,2048]{1,0:T(8,128)(2,1)} %bitcast.15, f32[1,2048]{1,0:T(1,128)} %bitcast.18, f32[1,2048]{1,0:T(1,128)} %bitcast.19, s32[3,16]{1,0:T(4,128)} %bitcast.20, s32[3,16]{1,0:T(4,128)} %bitcast.21, s32[3,16]{1,0:T(4,128)} %bitcast.22, bf16[2048,256]{1,0:T(8,128)(2,1)} %wq_hbm.1, ...), custom_call_target="tpu_custom_call" | custom-call | tf_op jit(solution)/shard_map/layer/pallas_call | solution.py:788
  142.5 1.5 %copy.20 = bf16[16,1,2048]{2,0,1:T(8,128)(2,1)} copy(bf16[16,1,2048]{2,0,1:T(8,128)(2,1)} %bitcast.14) | data formatting | bytes 131072

commit v6 on v5

--- a/solution.py
+++ b/solution.py
@@ -152,7 +152,7 @@
         self.passed = [to_lane(own, own, self.send.at[0], self.recv.at[0], p.sib)]
 
     def start(self):
-        for copy in self.direct + self.passed:
+        for copy in self.direct[3:] + self.direct[:3] + self.passed:
             copy.start()
 
     def finish(self):
@@ -363,7 +363,6 @@
     stacked = jnp.concatenate(
         [jnp.concatenate([queries, meta], axis=1) for meta in made["metas"]], axis=0
     )
-    qs[...] = nn_dot(made["places"], stacked).astype(BF).reshape(qs.shape)
 
     def q_copy(k):
         return to_group(qs.at[k], qr.at[k], q_send.at[k], q_recv.at[k], p.ahead(k))
@@ -371,7 +370,14 @@
     def b_copy(k):
         return to_group(bs.at[k], br.at[k], b_send.at[k], b_recv.at[k], p.behind(k))
 
-    each(1, groups, lambda k: q_copy(k).start())
+    some = groups // 2
+    for part in range(2):
+        begin = part * some
+        cut = slice(begin * slot_rows, (begin + some) * slot_rows)
+        qs[begin : begin + some] = (
+            nn_dot(made["places"][cut], stacked).astype(BF).reshape(some, *qs.shape[1:])
+        )
+        each(max(begin, 1), begin + some, lambda k: q_copy(k).start())
     qr[0] = qs[0]
 
     loads["wk"].wait()
@@ -501,7 +507,7 @@
         pick = (where == routes["slots"][0]).astype(F32)
         for k in range(1, top_count):
             pick = pick + (where == routes["slots"][k]).astype(F32)
-        row_picks.append(pick.astype(BF))
+        row_picks.append(nn_dot(pick.astype(BF), turn).astype(BF))
     each(1, groups, lambda k: b_copy(k).wait_recv())
     back_all = br[...].reshape(groups * slot_rows, br.shape[2])
     for level in range(3):
@@ -548,14 +554,16 @@
     x_own = []
     for s in range(PARTS):
         gathers[s].finish()
-        x = nn_dot(turn, rows2[s].reshape(tokens, span)).astype(BF)
-        x_own.append(x[:rows])
+        x = rows2[s].reshape(tokens, span)
         for c in range(chunks2):
             sb[s, c * per_chunk2 : (c + 1) * per_chunk2] = (
                 nn_dot(row_picks[c], x).astype(BF).reshape(per_chunk2, cap, span)
             )
             each(max(c * per_chunk2, 1), (c + 1) * per_chunk2, lambda k: d_copy(s, k).start())
         xb[s, 0] = sb[s, 0]
+        x_own.append(
+            nn_dot(turn[:rows, :rows], rows2[s, 0].reshape(rows, span)).astype(BF)
+        )
 
     loads["shin"].wait()
     loads["shout"].wait()

time: 145 us -> 145 us (level)
  no operation moved by 1% of the time
where the time goes in v6:
time: 145 us; the launch traced here: 144 us
  Pallas kernels  142 us (98%)
  local copies, waits for them, and re-layouts  1.47 us (1%)
    pallas_call x1, Pallas kernels, on_device(): pl.pallas_call(layer_kernel, out_shape=jax.ShapeDtypeStruct((requests, wi...  142 us

profile of v6, /device:TPU:32, one launch (start us, length us, event | category | flops | bytes accessed | tf_op | source)
XLA Modules:
  0.0 143.5 jit_solution(10149828576254930019)
XLA Ops:
  0.0 142.0 %layer.1 = bf16[16,2048]{1,0:T(8,128)(2,1)} custom-call(bf16[16,2048]{1,0:T(8,128)(2,1)} %bitcast.15, f32[1,2048]{1,0:T(1,128)} %bitcast.18, f32[1,2048]{1,0:T(1,128)} %bitcast.19, s32[3,16]{1,0:T(4,128)} %bitcast.20, s32[3,16]{1,0:T(4,128)} %bitcast.21, s32[3,16]{1,0:T(4,128)} %bitcast.22, bf16[2048,256]{1,0:T(8,128)(2,1)} %wq_hbm.1, ...), custom_call_target="tpu_custom_call" | custom-call | tf_op jit(solution)/shard_map/layer/pallas_call | solution.py:796
  142.1 1.5 %copy.20 = bf16[16,1,2048]{2,0,1:T(8,128)(2,1)} copy(bf16[16,1,2048]{2,0,1:T(8,128)(2,1)} %bitcast.14) | data formatting | bytes 131072
